TPU v7x, 512 devices: a whole 4x8x8 slice. The times are simulated.
512 devices in a mesh: stream: 8 (over z), span: 16 (over y, core), depth: 4 (over x).
Axes of the slice: x: 4, y: 8, z: 8, core: 2. Of those that a mesh axis runs over, the one named last changes fastest.
Arguments:
- forward_velocity: float32 [3, 64, 256, 512], P(None, 'stream', 'span', 'depth'), may hold values from -40 to 40, as said below
- adjoint_velocity: float32 [3, 64, 256, 512], P(None, 'stream', 'span', 'depth'), may hold values from -40 to 40, as said below
- weights: float32 [32, 81], replicated, may hold values from -0.625 to 0.625
Outputs:
- basis: float32 [32, 64, 256, 512], P(None, 'stream', 'span', 'depth')
Inputs may be any that keep to these rules, and one draw needn't show every extreme that they name: `forward_velocity`: a velocity field whose amplitude varies from cell to cell. `adjoint_velocity`: a velocity field whose amplitude varies from cell to cell.
All inputs are finite; a program needn't handle non-finite values.
Results may differ from a plain program's by a relative error of at most 0.0003.
Values sent between devices are 32-bit elements; how exact they have to be, the bound alone decides.
No kernel may reach another device: no remote copies, remote signals or barrier semaphores. Data moves between devices by JAX's collectives and lax.ppermute only.
A program may use at most 64 MiB of HBM per device.

v0:
```python
import jax
import jax.numpy as jnp
from jax import lax
from jax.sharding import PartitionSpec as P


def padded_2(shard, sides, width):
    for axis, dim in sides:
        size, length = (lax.axis_size(axis), shard.shape[dim])
        up = [(i, (i + 1) % size) for i in range(size)]
        down = [(j, i) for i, j in up]
        last = lax.slice_in_dim(shard, length - width, length, axis=dim)
        initial = lax.slice_in_dim(shard, 0, width, axis=dim)
        before = lax.ppermute(last, axis, up)
        after = lax.ppermute(initial, axis, down)
        shard = jnp.concatenate([before, shard, after], axis=dim)
    return shard


def partner_2(value, axis, stride):
    mask = 2**stride
    pairs = [(source, source ^ mask) for source in range(lax.axis_size(axis))]
    return lax.ppermute(value, axis, pairs)


def along_axis(field, axis, offset):
    parts = [slice(None), slice(None), slice(None), slice(None)]
    length = field.shape[axis]
    parts[axis] = slice(2 + offset, length - 2 + offset)
    return field[tuple(parts)]


def slope_along(padded, axis):
    near = along_axis(padded, axis, 1) - along_axis(padded, axis, -1)
    far = along_axis(padded, axis, 2) - along_axis(padded, axis, -2)
    return (8.0 * near - far) / 12.0


def snapshots(piece_x, piece_y, piece_z, weights):
    slopes = [slope_along(piece_x, 1), slope_along(piece_y, 2), slope_along(piece_z, 3)]
    stacked = jnp.stack(slopes, axis=1)
    grads = stacked.reshape(stacked.shape[0] * 3, -1)
    products = (grads[:9][:, None, :] * grads[9:][None, :, :]).reshape(81, -1)
    return jnp.dot(
        weights, products, precision=lax.Precision.HIGHEST, preferred_element_type=jnp.float32
    )


def inner(left, right):
    return jnp.dot(left, right, precision=lax.Precision.HIGHEST, preferred_element_type=jnp.float32)


def upper_factor(matrix):
    return jnp.linalg.cholesky(matrix).T


def body(forward_velocity, adjoint_velocity, weights):
    stacked = jnp.concatenate([forward_velocity, adjoint_velocity], 0)
    padded = padded_2(stacked, (("stream", 1), ("span", 2), ("depth", 3)), 2)
    padded_x = padded[:, :, 2:-2, 2:-2]
    padded_y = padded[:, 2:-2, :, 2:-2]
    padded_z = padded[:, 2:-2, 2:-2, :]
    planes, rows_y, rows_z = (
        forward_velocity.shape[1],
        forward_velocity.shape[2],
        forward_velocity.shape[3],
    )
    count_snap = weights.shape[0]
    step_planes = 2
    block_cells = step_planes * rows_y * rows_z

    def block_step(index, carry):
        snaps, gram = carry
        start = index * step_planes
        piece_x = lax.dynamic_slice_in_dim(padded_x, start, step_planes + 4, 1)
        piece_y = lax.dynamic_slice_in_dim(padded_y, start, step_planes, 1)
        piece_z = lax.dynamic_slice_in_dim(padded_z, start, step_planes, 1)
        block = snapshots(piece_x, piece_y, piece_z, weights)
        snaps = lax.dynamic_update_slice_in_dim(snaps, block, index * block_cells, 1)
        return (snaps, gram + inner(block, block.T))

    snaps = jnp.zeros((count_snap, planes * rows_y * rows_z), jnp.float32)
    gram = jnp.zeros((count_snap, count_snap), jnp.float32)
    snaps, gram = lax.fori_loop(0, planes // step_planes, block_step, (snaps, gram))
    devices_all = lax.axis_size("stream") * lax.axis_size("span") * lax.axis_size("depth")
    cells = planes * rows_y * rows_z * devices_all
    factor = upper_factor(gram)
    for bit in range(lax.axis_size(("stream", "span", "depth")).bit_length() - 1):
        partner = partner_2(factor, ("stream", "span", "depth"), bit)
        factor = upper_factor(inner(factor.T, factor) + inner(partner.T, partner))
    total = inner(factor.T, factor)
    lower = jnp.linalg.cholesky(total / cells)
    inverse = jax.scipy.linalg.solve_triangular(
        lower, jnp.eye(count_snap, dtype=jnp.float32), lower=True
    )
    basis = inner(inverse, snaps)
    return basis.reshape(count_snap, planes, rows_y, rows_z)


def solution(mesh):
    in_specs = (P(None, "stream", "span", "depth"), P(None, "stream", "span", "depth"), P())
    out_specs = P(None, "stream", "span", "depth")
    return jax.shard_map(body, mesh=mesh, in_specs=in_specs, out_specs=out_specs, check_vma=False)
```

profile of v0, /device:TPU:6, one launch (start us, length us, event | category | flops | bytes accessed | tf_op | source)
XLA Modules:
  0.0 183.6 jit_solution(333256461436282722)
XLA Ops:
  0.0 0.9 constant_dynamic-update-slice_fusion.1
  0.9 0.9 constant_dynamic-update-slice_fusion
  1.9 4.3 %collective-permute-start = (f32[6,2,16,128]{3,2,1,0:T(8,128)S(1)}, f32[6,2,16,128]{3,2,1,0:T(8,128)S(1)}, u32[]{:S(2)}, u32[]{:S(2)}) collective-permute-start(f32[6,2,16,128]{3,2,1,0:T(8,128)S(1)} %get-tuple-element.188), channel_id=1, source_target_pairs={{0,64},{64,128},{128,192},{192,256},{256,320},{320,384},{384,448},... | collective-permute-start | bytes 294920 | tf_op jit(solution)/shard_map/ppermute | solution.py:14
  6.2 8.6 %collective-permute-start.1 = (f32[6,2,16,128]{3,2,1,0:T(8,128)S(1)}, f32[6,2,16,128]{3,2,1,0:T(8,128)S(1)}, u32[]{:S(2)}, u32[]{:S(2)}) collective-permute-start(f32[6,2,16,128]{3,2,1,0:T(8,128)S(1)} %get-tuple-element.189), channel_id=1, source_target_pairs={{64,0},{128,64},{192,128},{256,192},{320,256},{384,320},{448,384},... | collective-permute-start | bytes 294920 | tf_op jit(solution)/shard_map/ppermute | solution.py:15
  14.8 0.8 collective-permute-done
  15.6 1.3 collective-permute-done.1
  17.1 2.9 %collective-permute-start.3 = (f32[6,12,2,128]{3,2,1,0:T(2,128)S(1)}, f32[6,12,2,128]{3,2,1,0:T(2,128)S(1)}, u32[]{:S(2)}, u32[]{:S(2)}) collective-permute-start(f32[6,12,2,128]{3,2,1,0:T(2,128)S(1)} %get-tuple-element.187), channel_id=1, source_target_pairs={{4,0},{8,4},{12,8},{16,12},{20,16},{24,20},{28,24},{32,28},{36,32}... | collective-permute-start | bytes 221192 | tf_op jit(solution)/shard_map/ppermute | solution.py:15
  20.1 2.0 %collective-permute-done.2 = f32[6,12,2,128]{3,2,1,0:T(2,128)S(1)} collective-permute-done((f32[6,12,2,128]{3,2,1,0:T(2,128)S(1)}, f32[6,12,2,128]{3,2,1,0:T(2,128)S(1)}, u32[]{:S(2)}, u32[]{:S(2)}) %collective-permute-start.2) | collective-permute-done | bytes 73760 | tf_op jit(solution)/shard_map/ppermute | solution.py:14
  23.5 1.2 fusion.117
  24.7 1.7 copy.158
  26.4 2.4 %collective-permute-start.4 = (f32[6,12,20,2]{2,3,1,0:T(2,128)S(1)}, f32[6,12,20,2]{2,3,1,0:T(2,128)S(1)}, u32[]{:S(2)}, u32[]{:S(2)}) collective-permute-start(f32[6,12,20,2]{2,3,1,0:T(2,128)S(1)} %copy.158), channel_id=1, source_target_pairs={{0,1},{1,2},{2,3},{3,0},{4,5},{5,6},{6,7},{7,4},{8,9},{9,10},{10,1... | collective-permute-start | bytes 34568 | tf_op jit(solution)/shard_map/ppermute | solution.py:14
  29.3 3.4 %collective-permute-start.5 = (f32[6,12,20,2]{2,3,1,0:T(2,128)S(1)}, f32[6,12,20,2]{2,3,1,0:T(2,128)S(1)}, u32[]{:S(2)}, u32[]{:S(2)}) collective-permute-start(f32[6,12,20,2]{2,3,1,0:T(2,128)S(1)} %copy.159), channel_id=1, source_target_pairs={{1,0},{2,1},{3,2},{0,3},{5,4},{6,5},{7,6},{4,7},{9,8},{10,9},{11,1... | collective-permute-start | bytes 34568 | tf_op jit(solution)/shard_map/ppermute | solution.py:15
  33.4 3.4 %collective-permute-done.5 = f32[6,12,20,2]{2,3,1,0:T(2,128)S(1)} collective-permute-done((f32[6,12,20,2]{2,3,1,0:T(2,128)S(1)}, f32[6,12,20,2]{2,3,1,0:T(2,128)S(1)}, u32[]{:S(2)}, u32[]{:S(2)}) %collective-permute-start.5) | collective-permute-done | bytes 11552 | tf_op jit(solution)/shard_map/ppermute | solution.py:15
  36.8 1.5 copy.108
  38.2 1.6 pad_maximum_fusion.2
  39.8 1.5 broadcast_in_dim.13
  41.2 26.2 %while.16 = (s32[]{:T(128)}, f32[32,16384]{1,0:T(8,128)}, f32[32,32]{1,0:T(8,128)S(1)}, f32[6,12,16,128]{3,2,1,0:T(8,128)S(1)}, f32[6,8,20,128]{3,2,1,0:T(8,128)...) while((s32[]{:T(128)}, f32[32,16384]{1,0:T(8,128)}, ...), condition=%wide.region_1.0_spmd.clone, body=%wide.region_0.0_spmd.clone.sunk | while | flops 178583568 | bytes 18319992 | solution.py:84
  42.6 1.3 mul.118
  43.9 3.3 %bitcast_dynamic-update-slice_fusion.2 = (f32[32,16384]{1,0:T(8,128)}, f32[4096,32]{0,1:T(8,128)S(1)}) fusion(f32[32,16384]{1,0:T(8,128)} %get-tuple-element.263, s32[]{:T(128)S(6)} %select_n.93, f32[81,4096]{1,0:T(8,128)} %mul.118, f32[32,81]{1,0:T(8,128)S(1)} %get-tuple-element.285), kind=kOutput, calls=%fused_computation.2.clone.1 | convolution fusion | flops 127401984 | bytes 2500740 | tf_op jit(solution)/shard_map/while/body/eval_jaxpr/dot_general | solution.py:44
  49.2 1.3 mul.118
  50.5 3.3 %bitcast_dynamic-update-slice_fusion.2 = (f32[32,16384]{1,0:T(8,128)}, f32[4096,32]{0,1:T(8,128)S(1)}) fusion(f32[32,16384]{1,0:T(8,128)} %get-tuple-element.263, s32[]{:T(128)S(6)} %select_n.93, f32[81,4096]{1,0:T(8,128)} %mul.118, f32[32,81]{1,0:T(8,128)S(1)} %get-tuple-element.285), kind=kOutput, calls=%fused_computation.2.clone.1 | convolution fusion | flops 127401984 | bytes 2500740 | tf_op jit(solution)/shard_map/while/body/eval_jaxpr/dot_general | solution.py:44
  55.7 1.3 mul.118
  57.1 3.3 %bitcast_dynamic-update-slice_fusion.2 = (f32[32,16384]{1,0:T(8,128)}, f32[4096,32]{0,1:T(8,128)S(1)}) fusion(f32[32,16384]{1,0:T(8,128)} %get-tuple-element.263, s32[]{:T(128)S(6)} %select_n.93, f32[81,4096]{1,0:T(8,128)} %mul.118, f32[32,81]{1,0:T(8,128)S(1)} %get-tuple-element.285), kind=kOutput, calls=%fused_computation.2.clone.1 | convolution fusion | flops 127401984 | bytes 2500740 | tf_op jit(solution)/shard_map/while/body/eval_jaxpr/dot_general | solution.py:44
  62.3 1.3 mul.118
  63.6 3.3 %bitcast_dynamic-update-slice_fusion.2 = (f32[32,16384]{1,0:T(8,128)}, f32[4096,32]{0,1:T(8,128)S(1)}) fusion(f32[32,16384]{1,0:T(8,128)} %get-tuple-element.263, s32[]{:T(128)S(6)} %select_n.93, f32[81,4096]{1,0:T(8,128)} %mul.118, f32[32,81]{1,0:T(8,128)S(1)} %get-tuple-element.285), kind=kOutput, calls=%fused_computation.2.clone.1 | convolution fusion | flops 127401984 | bytes 2500740 | tf_op jit(solution)/shard_map/while/body/eval_jaxpr/dot_general | solution.py:44
  67.6 2.9 %cholesky.179 = f32[32,32]{1,0:T(8,128)S(1)} custom-call(f32[32,32]{1,0:T(8,128)S(1)} %fusion.25), custom_call_target="Cholesky" | custom-call | tf_op jit(solution)/shard_map/jit(cholesky)/cholesky | solution.py:54
  72.0 2.2 %collective-permute-start.6 = (f32[32,32]{0,1:T(8,128)S(1)}, f32[32,32]{0,1:T(8,128)S(1)}, u32[]{:S(2)}, u32[]{:S(2)}) collective-permute-start(f32[32,32]{0,1:T(8,128)S(1)} %fusion.48), channel_id=1, source_target_pairs={{0,1},{1,0},{2,3},{3,2},{4,5},{5,4},{6,7},{7,6},{8,9},{9,8},{10,11... | collective-permute-start | bytes 12296 | tf_op jit(solution)/shard_map/ppermute | solution.py:23
  74.2 0.8 fusion.49
  75.0 2.5 %collective-permute-done.6 = f32[32,32]{0,1:T(8,128)S(1)} collective-permute-done((f32[32,32]{0,1:T(8,128)S(1)}, f32[32,32]{0,1:T(8,128)S(1)}, u32[]{:S(2)}, u32[]{:S(2)}) %collective-permute-start.6) | collective-permute-done | bytes 4128 | tf_op jit(solution)/shard_map/ppermute | solution.py:23
  77.8 2.9 %cholesky.190 = f32[32,32]{1,0:T(8,128)S(1)} custom-call(f32[32,32]{1,0:T(8,128)S(1)} %fusion.24), custom_call_target="Cholesky" | custom-call | tf_op jit(solution)/shard_map/jit(cholesky)/cholesky | solution.py:54
  82.2 3.1 %collective-permute-start.7 = (f32[32,32]{0,1:T(8,128)S(1)}, f32[32,32]{0,1:T(8,128)S(1)}, u32[]{:S(2)}, u32[]{:S(2)}) collective-permute-start(f32[32,32]{0,1:T(8,128)S(1)} %fusion.50), channel_id=1, source_target_pairs={{0,2},{1,3},{2,0},{3,1},{4,6},{5,7},{6,4},{7,5},{8,10},{9,11},{10,... | collective-permute-start | bytes 12296 | tf_op jit(solution)/shard_map/ppermute | solution.py:23
  85.3 0.8 fusion.51
  86.2 3.2 %collective-permute-done.7 = f32[32,32]{0,1:T(8,128)S(1)} collective-permute-done((f32[32,32]{0,1:T(8,128)S(1)}, f32[32,32]{0,1:T(8,128)S(1)}, u32[]{:S(2)}, u32[]{:S(2)}) %collective-permute-start.7) | collective-permute-done | bytes 4128 | tf_op jit(solution)/shard_map/ppermute | solution.py:23
  89.6 2.9 %cholesky.201 = f32[32,32]{1,0:T(8,128)S(1)} custom-call(f32[32,32]{1,0:T(8,128)S(1)} %fusion.23), custom_call_target="Cholesky" | custom-call | tf_op jit(solution)/shard_map/jit(cholesky)/cholesky | solution.py:54
  94.0 1.9 %collective-permute-start.8 = (f32[32,32]{0,1:T(8,128)S(1)}, f32[32,32]{0,1:T(8,128)S(1)}, u32[]{:S(2)}, u32[]{:S(2)}) collective-permute-start(f32[32,32]{0,1:T(8,128)S(1)} %fusion.52), channel_id=1, source_target_pairs={{0,4},{1,5},{2,6},{3,7},{4,0},{5,1},{6,2},{7,3},{8,12},{9,13},{10,... | collective-permute-start | bytes 12296 | tf_op jit(solution)/shard_map/ppermute | solution.py:23
  95.9 0.8 fusion.53
  97.3 2.9 %cholesky.212 = f32[32,32]{1,0:T(8,128)S(1)} custom-call(f32[32,32]{1,0:T(8,128)S(1)} %fusion.22), custom_call_target="Cholesky" | custom-call | tf_op jit(solution)/shard_map/jit(cholesky)/cholesky | solution.py:54
  101.7 2.9 %collective-permute-start.9 = (f32[32,32]{0,1:T(8,128)S(1)}, f32[32,32]{0,1:T(8,128)S(1)}, u32[]{:S(2)}, u32[]{:S(2)}) collective-permute-start(f32[32,32]{0,1:T(8,128)S(1)} %fusion.54), channel_id=1, source_target_pairs={{0,8},{1,9},{2,10},{3,11},{4,12},{5,13},{6,14},{7,15},{8,0},{9,1},... | collective-permute-start | bytes 12296 | tf_op jit(solution)/shard_map/ppermute | solution.py:23
  104.5 0.8 fusion.55
  105.4 1.9 %collective-permute-done.9 = f32[32,32]{0,1:T(8,128)S(1)} collective-permute-done((f32[32,32]{0,1:T(8,128)S(1)}, f32[32,32]{0,1:T(8,128)S(1)}, u32[]{:S(2)}, u32[]{:S(2)}) %collective-permute-start.9) | collective-permute-done | bytes 4128 | tf_op jit(solution)/shard_map/ppermute | solution.py:23
  107.5 2.9 %cholesky.223 = f32[32,32]{1,0:T(8,128)S(1)} custom-call(f32[32,32]{1,0:T(8,128)S(1)} %fusion.21), custom_call_target="Cholesky" | custom-call | tf_op jit(solution)/shard_map/jit(cholesky)/cholesky | solution.py:54
  111.9 3.9 %collective-permute-start.10 = (f32[32,32]{0,1:T(8,128)S(1)}, f32[32,32]{0,1:T(8,128)S(1)}, u32[]{:S(2)}, u32[]{:S(2)}) collective-permute-start(f32[32,32]{0,1:T(8,128)S(1)} %fusion.56), channel_id=1, source_target_pairs={{0,16},{1,17},{2,18},{3,19},{4,20},{5,21},{6,22},{7,23},{8,24},{9,... | collective-permute-start | bytes 12296 | tf_op jit(solution)/shard_map/ppermute | solution.py:23
  115.8 0.8 fusion.57
  116.7 1.8 collective-permute-done.10
  118.7 2.9 %cholesky.234 = f32[32,32]{1,0:T(8,128)S(1)} custom-call(f32[32,32]{1,0:T(8,128)S(1)} %fusion.20), custom_call_target="Cholesky" | custom-call | tf_op jit(solution)/shard_map/jit(cholesky)/cholesky | solution.py:54
  123.1 7.7 %collective-permute-start.11 = (f32[32,32]{0,1:T(8,128)S(1)}, f32[32,32]{0,1:T(8,128)S(1)}, u32[]{:S(2)}, u32[]{:S(2)}) collective-permute-start(f32[32,32]{0,1:T(8,128)S(1)} %fusion.58), channel_id=1, source_target_pairs={{0,32},{1,33},{2,34},{3,35},{4,36},{5,37},{6,38},{7,39},{8,40},{9,... | collective-permute-start | bytes 12296 | tf_op jit(solution)/shard_map/ppermute | solution.py:23
  131.6 1.0 collective-permute-done.11
  132.8 2.9 %cholesky.245 = f32[32,32]{1,0:T(8,128)S(1)} custom-call(f32[32,32]{1,0:T(8,128)S(1)} %fusion.19), custom_call_target="Cholesky" | custom-call | tf_op jit(solution)/shard_map/jit(cholesky)/cholesky | solution.py:54
  137.2 1.9 %collective-permute-start.12 = (f32[32,32]{0,1:T(8,128)S(1)}, f32[32,32]{0,1:T(8,128)S(1)}, u32[]{:S(2)}, u32[]{:S(2)}) collective-permute-start(f32[32,32]{0,1:T(8,128)S(1)} %fusion.60), channel_id=1, source_target_pairs={{0,64},{1,65},{2,66},{3,67},{4,68},{5,69},{6,70},{7,71},{8,72},{9,... | collective-permute-start | bytes 12296 | tf_op jit(solution)/shard_map/ppermute | solution.py:23
  139.1 0.8 fusion.61
  140.0 2.9 %collective-permute-done.12 = f32[32,32]{0,1:T(8,128)S(1)} collective-permute-done((f32[32,32]{0,1:T(8,128)S(1)}, f32[32,32]{0,1:T(8,128)S(1)}, u32[]{:S(2)}, u32[]{:S(2)}) %collective-permute-start.12) | collective-permute-done | bytes 4128 | tf_op jit(solution)/shard_map/ppermute | solution.py:23
  143.1 2.9 %cholesky.256 = f32[32,32]{1,0:T(8,128)S(1)} custom-call(f32[32,32]{1,0:T(8,128)S(1)} %fusion.18), custom_call_target="Cholesky" | custom-call | tf_op jit(solution)/shard_map/jit(cholesky)/cholesky | solution.py:54
  147.5 4.6 %collective-permute-start.13 = (f32[32,32]{0,1:T(8,128)S(1)}, f32[32,32]{0,1:T(8,128)S(1)}, u32[]{:S(2)}, u32[]{:S(2)}) collective-permute-start(f32[32,32]{0,1:T(8,128)S(1)} %fusion.62), channel_id=1, source_target_pairs={{0,128},{1,129},{2,130},{3,131},{4,132},{5,133},{6,134},{7,135},{8... | collective-permute-start | bytes 12296 | tf_op jit(solution)/shard_map/ppermute | solution.py:23
  152.9 1.1 collective-permute-done.13
  154.2 2.9 %cholesky.267 = f32[32,32]{1,0:T(8,128)S(1)} custom-call(f32[32,32]{1,0:T(8,128)S(1)} %fusion.17), custom_call_target="Cholesky" | custom-call | tf_op jit(solution)/shard_map/jit(cholesky)/cholesky | solution.py:54
  158.6 5.9 %collective-permute-start.14 = (f32[32,32]{0,1:T(8,128)S(1)}, f32[32,32]{0,1:T(8,128)S(1)}, u32[]{:S(2)}, u32[]{:S(2)}) collective-permute-start(f32[32,32]{0,1:T(8,128)S(1)} %fusion.64), channel_id=1, source_target_pairs={{0,256},{1,257},{2,258},{3,259},{4,260},{5,261},{6,262},{7,263},{8... | collective-permute-start | bytes 12296 | tf_op jit(solution)/shard_map/ppermute | solution.py:23
  164.5 0.8 fusion.65
  165.4 2.8 %collective-permute-done.14 = f32[32,32]{0,1:T(8,128)S(1)} collective-permute-done((f32[32,32]{0,1:T(8,128)S(1)}, f32[32,32]{0,1:T(8,128)S(1)}, u32[]{:S(2)}, u32[]{:S(2)}) %collective-permute-start.14) | collective-permute-done | bytes 4128 | tf_op jit(solution)/shard_map/ppermute | solution.py:23
  168.4 2.9 %cholesky.278 = f32[32,32]{1,0:T(8,128)S(1)} custom-call(f32[32,32]{1,0:T(8,128)S(1)} %fusion.16), custom_call_target="Cholesky" | custom-call | tf_op jit(solution)/shard_map/jit(cholesky)/cholesky | solution.py:54
  172.1 0.8 convolution_multiply_fusion
  173.0 2.9 %cholesky.289 = f32[32,32]{1,0:T(8,128)S(1)} custom-call(f32[32,32]{1,0:T(8,128)S(1)} %fusion.15), custom_call_target="Cholesky" | custom-call | tf_op jit(solution)/shard_map/jit(cholesky)/cholesky | solution.py:92
  177.4 2.4 %custom-call.6 = f32[1,32,32]{1,2,0:T(8,128)S(1)} custom-call(f32[1,32,32]{2,1,0:T(8,128)S(1)} %fusion.12), custom_call_target="InvertDiagBlocksLowerTriangular" | custom-call | tf_op jit(solution)/shard_map/jit(_solve_triangular)/triangular_solve | solution.py:93
  180.0 1.9 %convolution_bitcast_fusion = f32[4,8,128,128]{3,1,2,0:T(8,128)S(1)} fusion(f32[32,32]{1,0:T(8,128)S(1)} %fusion.13, f32[32,16384]{1,0:T(8,128)S(1)} %copy-done.4), kind=kOutput, calls=%fused_computation.22 | convolution fusion | flops 201326592 | bytes 4198400 | tf_op jit(solution)/shard_map/dot_general | solution.py:50
  182.0 1.7 copy.160
  (158 shorter events, 29.7 us)
Async XLA Ops:
  1.9 13.7 %collective-permute-start = (f32[6,2,16,128]{3,2,1,0:T(8,128)S(1)}, f32[6,2,16,128]{3,2,1,0:T(8,128)S(1)}, u32[]{:S(2)}, u32[]{:S(2)}) collective-permute-start(f32[6,2,16,128]{3,2,1,0:T(8,128)S(1)} %get-tuple-element.188), channel_id=1, source_target_pairs={{0,64},{64,128},{128,192},{192,256},{256,320},{320,384},{384,448},... | collective-permute-start | bytes 294920 | tf_op jit(solution)/shard_map/ppermute | solution.py:14
  6.2 10.8 %collective-permute-start.1 = (f32[6,2,16,128]{3,2,1,0:T(8,128)S(1)}, f32[6,2,16,128]{3,2,1,0:T(8,128)S(1)}, u32[]{:S(2)}, u32[]{:S(2)}) collective-permute-start(f32[6,2,16,128]{3,2,1,0:T(8,128)S(1)} %get-tuple-element.189), channel_id=1, source_target_pairs={{64,0},{128,64},{192,128},{256,192},{320,256},{384,320},{448,384},... | collective-permute-start | bytes 294920 | tf_op jit(solution)/shard_map/ppermute | solution.py:15
  17.1 5.0 %collective-permute-start.2 = (f32[6,12,2,128]{3,2,1,0:T(2,128)S(1)}, f32[6,12,2,128]{3,2,1,0:T(2,128)S(1)}, u32[]{:S(2)}, u32[]{:S(2)}) collective-permute-start(f32[6,12,2,128]{3,2,1,0:T(2,128)S(1)} %get-tuple-element.186), channel_id=1, source_target_pairs={{0,4},{4,8},{8,12},{12,16},{16,20},{20,24},{24,28},{28,32},{32,36}... | collective-permute-start | bytes 221192 | tf_op jit(solution)/shard_map/ppermute | solution.py:14
  17.1 5.0 %collective-permute-start.3 = (f32[6,12,2,128]{3,2,1,0:T(2,128)S(1)}, f32[6,12,2,128]{3,2,1,0:T(2,128)S(1)}, u32[]{:S(2)}, u32[]{:S(2)}) collective-permute-start(f32[6,12,2,128]{3,2,1,0:T(2,128)S(1)} %get-tuple-element.187), channel_id=1, source_target_pairs={{4,0},{8,4},{12,8},{16,12},{20,16},{24,20},{28,24},{32,28},{36,32}... | collective-permute-start | bytes 221192 | tf_op jit(solution)/shard_map/ppermute | solution.py:15
  22.1 0.6 copy-start.6
  22.7 0.6 copy-start.7
  26.4 6.4 %collective-permute-start.4 = (f32[6,12,20,2]{2,3,1,0:T(2,128)S(1)}, f32[6,12,20,2]{2,3,1,0:T(2,128)S(1)}, u32[]{:S(2)}, u32[]{:S(2)}) collective-permute-start(f32[6,12,20,2]{2,3,1,0:T(2,128)S(1)} %copy.158), channel_id=1, source_target_pairs={{0,1},{1,2},{2,3},{3,0},{4,5},{5,6},{6,7},{7,4},{8,9},{9,10},{10,1... | collective-permute-start | bytes 34568 | tf_op jit(solution)/shard_map/ppermute | solution.py:14
  29.3 7.4 %collective-permute-start.5 = (f32[6,12,20,2]{2,3,1,0:T(2,128)S(1)}, f32[6,12,20,2]{2,3,1,0:T(2,128)S(1)}, u32[]{:S(2)}, u32[]{:S(2)}) collective-permute-start(f32[6,12,20,2]{2,3,1,0:T(2,128)S(1)} %copy.159), channel_id=1, source_target_pairs={{1,0},{2,1},{3,2},{0,3},{5,4},{6,5},{7,6},{4,7},{9,8},{10,9},{11,1... | collective-permute-start | bytes 34568 | tf_op jit(solution)/shard_map/ppermute | solution.py:15
  38.2 3.0 %copy-start.5 = (f32[32,81]{1,0:T(8,128)S(1)}, f32[32,81]{1,0:T(8,128)}, u32[]{:S(2)}) copy-start(f32[32,81]{1,0:T(8,128)} %param.8) | copy-start | bytes 31108
  41.3 0.8 copy-start
  41.3 1.1 copy-start.2
  43.9 3.9 %copy-start.1 = (f32[6,8,20,128]{3,2,1,0:T(8,128)S(1)}, f32[6,8,20,128]{3,2,1,0:T(8,128)}, u32[]{:S(2)}) copy-start(f32[6,8,20,128]{3,2,1,0:T(8,128)} %copy-done) | copy-start | bytes 1474564 | tf_op jit(solution)/shard_map/while
  43.9 3.9 %copy-start.3 = (f32[6,8,16,132]{3,2,1,0:T(8,128)S(1)}, f32[6,8,16,132]{3,2,1,0:T(8,128)}, u32[]{:S(2)}) copy-start(f32[6,8,16,132]{3,2,1,0:T(8,128)} %copy-done.2) | copy-start | bytes 1216516 | tf_op jit(solution)/shard_map/while
  47.8 0.8 copy-start
  47.8 1.1 copy-start.2
  50.5 3.9 %copy-start.1 = (f32[6,8,20,128]{3,2,1,0:T(8,128)S(1)}, f32[6,8,20,128]{3,2,1,0:T(8,128)}, u32[]{:S(2)}) copy-start(f32[6,8,20,128]{3,2,1,0:T(8,128)} %copy-done) | copy-start | bytes 1474564 | tf_op jit(solution)/shard_map/while
  50.5 3.9 %copy-start.3 = (f32[6,8,16,132]{3,2,1,0:T(8,128)S(1)}, f32[6,8,16,132]{3,2,1,0:T(8,128)}, u32[]{:S(2)}) copy-start(f32[6,8,16,132]{3,2,1,0:T(8,128)} %copy-done.2) | copy-start | bytes 1216516 | tf_op jit(solution)/shard_map/while
  54.4 0.8 copy-start
  54.4 1.1 copy-start.2
  57.0 3.9 %copy-start.1 = (f32[6,8,20,128]{3,2,1,0:T(8,128)S(1)}, f32[6,8,20,128]{3,2,1,0:T(8,128)}, u32[]{:S(2)}) copy-start(f32[6,8,20,128]{3,2,1,0:T(8,128)} %copy-done) | copy-start | bytes 1474564 | tf_op jit(solution)/shard_map/while
  57.0 3.9 %copy-start.3 = (f32[6,8,16,132]{3,2,1,0:T(8,128)S(1)}, f32[6,8,16,132]{3,2,1,0:T(8,128)}, u32[]{:S(2)}) copy-start(f32[6,8,16,132]{3,2,1,0:T(8,128)} %copy-done.2) | copy-start | bytes 1216516 | tf_op jit(solution)/shard_map/while
  60.9 0.8 copy-start
  60.9 1.1 copy-start.2
  63.6 3.9 %copy-start.1 = (f32[6,8,20,128]{3,2,1,0:T(8,128)S(1)}, f32[6,8,20,128]{3,2,1,0:T(8,128)}, u32[]{:S(2)}) copy-start(f32[6,8,20,128]{3,2,1,0:T(8,128)} %copy-done) | copy-start | bytes 1474564 | tf_op jit(solution)/shard_map/while
  63.6 3.9 %copy-start.3 = (f32[6,8,16,132]{3,2,1,0:T(8,128)S(1)}, f32[6,8,16,132]{3,2,1,0:T(8,128)}, u32[]{:S(2)}) copy-start(f32[6,8,16,132]{3,2,1,0:T(8,128)} %copy-done.2) | copy-start | bytes 1216516 | tf_op jit(solution)/shard_map/while
  67.5 112.5 %copy-start.4 = (f32[32,16384]{1,0:T(8,128)S(1)}, f32[32,16384]{1,0:T(8,128)}, u32[]{:S(2)}) copy-start(f32[32,16384]{1,0:T(8,128)} %get-tuple-element.132) | copy-start | bytes 6291460
  72.0 5.6 %collective-permute-start.6 = (f32[32,32]{0,1:T(8,128)S(1)}, f32[32,32]{0,1:T(8,128)S(1)}, u32[]{:S(2)}, u32[]{:S(2)}) collective-permute-start(f32[32,32]{0,1:T(8,128)S(1)} %fusion.48), channel_id=1, source_target_pairs={{0,1},{1,0},{2,3},{3,2},{4,5},{5,4},{6,7},{7,6},{8,9},{9,8},{10,11... | collective-permute-start | bytes 12296 | tf_op jit(solution)/shard_map/ppermute | solution.py:23
  82.2 7.1 %collective-permute-start.7 = (f32[32,32]{0,1:T(8,128)S(1)}, f32[32,32]{0,1:T(8,128)S(1)}, u32[]{:S(2)}, u32[]{:S(2)}) collective-permute-start(f32[32,32]{0,1:T(8,128)S(1)} %fusion.50), channel_id=1, source_target_pairs={{0,2},{1,3},{2,0},{3,1},{4,6},{5,7},{6,4},{7,5},{8,10},{9,11},{10,... | collective-permute-start | bytes 12296 | tf_op jit(solution)/shard_map/ppermute | solution.py:23
  94.0 3.1 %collective-permute-start.8 = (f32[32,32]{0,1:T(8,128)S(1)}, f32[32,32]{0,1:T(8,128)S(1)}, u32[]{:S(2)}, u32[]{:S(2)}) collective-permute-start(f32[32,32]{0,1:T(8,128)S(1)} %fusion.52), channel_id=1, source_target_pairs={{0,4},{1,5},{2,6},{3,7},{4,0},{5,1},{6,2},{7,3},{8,12},{9,13},{10,... | collective-permute-start | bytes 12296 | tf_op jit(solution)/shard_map/ppermute | solution.py:23
  101.7 5.6 %collective-permute-start.9 = (f32[32,32]{0,1:T(8,128)S(1)}, f32[32,32]{0,1:T(8,128)S(1)}, u32[]{:S(2)}, u32[]{:S(2)}) collective-permute-start(f32[32,32]{0,1:T(8,128)S(1)} %fusion.54), channel_id=1, source_target_pairs={{0,8},{1,9},{2,10},{3,11},{4,12},{5,13},{6,14},{7,15},{8,0},{9,1},... | collective-permute-start | bytes 12296 | tf_op jit(solution)/shard_map/ppermute | solution.py:23
  111.9 6.5 %collective-permute-start.10 = (f32[32,32]{0,1:T(8,128)S(1)}, f32[32,32]{0,1:T(8,128)S(1)}, u32[]{:S(2)}, u32[]{:S(2)}) collective-permute-start(f32[32,32]{0,1:T(8,128)S(1)} %fusion.56), channel_id=1, source_target_pairs={{0,16},{1,17},{2,18},{3,19},{4,20},{5,21},{6,22},{7,23},{8,24},{9,... | collective-permute-start | bytes 12296 | tf_op jit(solution)/shard_map/ppermute | solution.py:23
  123.1 9.6 %collective-permute-start.11 = (f32[32,32]{0,1:T(8,128)S(1)}, f32[32,32]{0,1:T(8,128)S(1)}, u32[]{:S(2)}, u32[]{:S(2)}) collective-permute-start(f32[32,32]{0,1:T(8,128)S(1)} %fusion.58), channel_id=1, source_target_pairs={{0,32},{1,33},{2,34},{3,35},{4,36},{5,37},{6,38},{7,39},{8,40},{9,... | collective-permute-start | bytes 12296 | tf_op jit(solution)/shard_map/ppermute | solution.py:23
  137.2 5.6 %collective-permute-start.12 = (f32[32,32]{0,1:T(8,128)S(1)}, f32[32,32]{0,1:T(8,128)S(1)}, u32[]{:S(2)}, u32[]{:S(2)}) collective-permute-start(f32[32,32]{0,1:T(8,128)S(1)} %fusion.60), channel_id=1, source_target_pairs={{0,64},{1,65},{2,66},{3,67},{4,68},{5,69},{6,70},{7,71},{8,72},{9,... | collective-permute-start | bytes 12296 | tf_op jit(solution)/shard_map/ppermute | solution.py:23
  147.5 6.5 %collective-permute-start.13 = (f32[32,32]{0,1:T(8,128)S(1)}, f32[32,32]{0,1:T(8,128)S(1)}, u32[]{:S(2)}, u32[]{:S(2)}) collective-permute-start(f32[32,32]{0,1:T(8,128)S(1)} %fusion.62), channel_id=1, source_target_pairs={{0,128},{1,129},{2,130},{3,131},{4,132},{5,133},{6,134},{7,135},{8... | collective-permute-start | bytes 12296 | tf_op jit(solution)/shard_map/ppermute | solution.py:23
  158.6 9.5 %collective-permute-start.14 = (f32[32,32]{0,1:T(8,128)S(1)}, f32[32,32]{0,1:T(8,128)S(1)}, u32[]{:S(2)}, u32[]{:S(2)}) collective-permute-start(f32[32,32]{0,1:T(8,128)S(1)} %fusion.64), channel_id=1, source_target_pairs={{0,256},{1,257},{2,258},{3,259},{4,260},{5,261},{6,262},{7,263},{8... | collective-permute-start | bytes 12296 | tf_op jit(solution)/shard_map/ppermute | solution.py:23
where the time goes:
time: 185 us; the launch traced here: 184 us
  starting transfers between devices  55.9 us (30%)
  other arithmetic  53.5 us (29%)
  matrix products  27.1 us (15%)
  waiting for transfers between devices  25 us (14%)
  local copies, waits for them, and re-layouts  21.2 us (11%)
    another operation x30, other arithmetic, upper_factor(): return jnp.linalg.cholesky(matrix).T  36.8 us
    ppermute x9, starting transfers between devices, partner_2(): return lax.ppermute(value, axis, pairs)  34.2 us
    ppermute x9, waiting for transfers between devices, partner_2(): return lax.ppermute(value, axis, pairs)  17.4 us
    ppermute x3, starting transfers between devices, padded_2(): after = lax.ppermute(initial, axis, down)  15 us
    dot_general x24, matrix products, inner(): jnp.dot(left, right, precision=lax.Precision.HIGHEST, preferred_element_t...  13.8 us
    dot_general x4, matrix products, snapshots(): jnp.dot(weights, products, precision=lax.Precision.HIGHEST, preferred_ele...  13.1 us
    ppermute x3, starting transfers between devices, padded_2(): before = lax.ppermute(last, axis, up)  6.67 us
    transpose x9, other arithmetic, upper_factor(): return jnp.linalg.cholesky(matrix).T  6.24 us
  transfers between devices with their start and end apart: 15, of which 13 were waited for; matrix products, arithmetic and copies ran while one was open for 5% of the time, Pallas kernels for 0%

commit v1 on v0

v1 whole, which is shorter than its diff:
```python
import functools

import jax
import jax.numpy as jnp
from jax import lax
from jax.experimental import pallas as pl
from jax.experimental.pallas import tpu as pltpu
from jax.sharding import PartitionSpec as P

F32 = jnp.float32
BF16 = jnp.bfloat16
INTERPRET = False
VMEM = pl.BlockSpec(memory_space=pltpu.VMEM)
GROUP = 82 * 8
DEPTH = 2048


def iota(shape, dim):
    return lax.broadcasted_iota(jnp.int32, shape, dim)


def split(value):
    high = value.astype(BF16)
    low = (value - high.astype(F32)).astype(BF16)
    return high, low


def dot(left, right):
    return jnp.dot(left, right, preferred_element_type=F32)


def dot_nt(left, right):
    return lax.dot_general(left, right, (((1,), (1,)), ((), ())), preferred_element_type=F32)


def place(index):
    return divmod(index * 4, 128)


def sends_kernel(f_ref, a_ref, xf, xl, yf, yl, zs):
    planes, rows = f_ref.shape[1], f_ref.shape[2]
    for ref, base in ((f_ref, 0), (a_ref, 3)):
        part = slice(base, base + 3)
        xf[part] = ref[:, 0:2]
        xl[part] = ref[:, planes - 2 : planes]
        yf[part] = ref[:, :, 0:2, :]
        yl[part] = ref[:, :, rows - 2 : rows, :]
    lane = iota((8, 128), 1)
    packed = [jnp.zeros((8, 128), F32) for _ in range(zs.shape[0] // 8)]
    for comp in range(6):
        ref = f_ref if comp < 3 else a_ref
        for plane in range(planes):
            for half in range(rows // 8):
                group, at = place((comp * planes + plane) * (rows // 8) + half)
                tile = ref[comp % 3, plane, 8 * half : 8 * half + 8, :]
                moved = pltpu.roll(tile, (2 + at) % 128, 1)
                here = (lane >= at) & (lane < at + 4)
                packed[group] = jnp.where(here, moved, packed[group])
    for group, tile in enumerate(packed):
        zs[8 * group : 8 * group + 8, :] = tile


def weights_kernel(w_ref, wk_ref):
    pairs = w_ref.shape[1]
    high, low = split(w_ref[...] * (1.0 / 144.0))
    q = iota((pairs, DEPTH), 1)
    p = iota((pairs, DEPTH), 0)
    r = jnp.where(q >= GROUP, q - GROUP, q)
    r = jnp.where(r >= GROUP, r - GROUP, r)
    hit = lax.shift_right_logical(r, 3) == p
    to_high = jnp.where(hit & (q < 2 * GROUP), 1.0, 0.0).astype(BF16)
    to_low = jnp.where(hit & (q >= 2 * GROUP) & (q < 3 * GROUP), 1.0, 0.0).astype(BF16)
    wide = (dot(high, to_high) + dot(low, to_low)).astype(BF16)
    wk_ref[...] = spread(wide)


def spread(wide):
    snaps, n = wide.shape
    rows = 8 * snaps
    e = (lax.shift_right_logical(iota((rows, snaps), 0), 3) == iota((rows, snaps), 1))
    tall = dot(jnp.where(e, 1.0, 0.0).astype(BF16), wide)
    same = (iota((rows, n), 0) & 7) == (iota((rows, n), 1) & 7)
    return jnp.where(same, tall, 0.0).astype(BF16)


def compute_kernel(f_ref, a_ref, xb, xa, yb, ya, zb, za, wk_ref, sh_ref, sl_ref, g_ref, ypad):
    planes, rows = f_ref.shape[1], f_ref.shape[2]
    halves = rows // 8
    lane = iota((8, 128), 1)
    total = None
    for comp in range(6):
        ref = f_ref if comp < 3 else a_ref
        for plane in range(planes):
            ypad[comp, plane, 8 : 8 + rows, :] = ref[comp % 3, plane]
    ypad[:, :, 6:8, :] = yb[...]
    ypad[:, :, 8 + rows : 10 + rows, :] = ya[...]

    def line(comp, plane):
        if plane < 0:
            return xb[comp, plane + 2]
        if plane >= planes:
            return xa[comp, plane - planes]
        return (f_ref if comp < 3 else a_ref)[comp % 3, plane]

    def depth_slope(comp, plane, half):
        tile = ypad[comp, plane, 8 + 8 * half : 16 + 8 * half, :]
        group, at = place((comp * planes + plane) * halves + half)
        before = zb[8 * group : 8 * group + 8, :]
        after = za[8 * group : 8 * group + 8, :]
        up1 = jnp.where(lane < 1, pltpu.roll(before, (127 - at) % 128, 1), pltpu.roll(tile, 1, 1))
        up2 = jnp.where(lane < 2, pltpu.roll(before, (128 - at) % 128, 1), pltpu.roll(tile, 2, 1))
        dn1 = jnp.where(lane >= 127, pltpu.roll(after, (125 - at) % 128, 1), pltpu.roll(tile, 127, 1))
        dn2 = jnp.where(lane >= 126, pltpu.roll(after, (124 - at) % 128, 1), pltpu.roll(tile, 126, 1))
        return 8.0 * (dn1 - up1) - (dn2 - up2)

    for plane in range(planes):
        slopes = []
        for comp in range(6):
            dx = 8.0 * (line(comp, plane + 1) - line(comp, plane - 1)) - (
                line(comp, plane + 2) - line(comp, plane - 2)
            )
            y = lambda k: ypad[comp, plane, 8 + k : 8 + k + rows, :]
            dy = 8.0 * (y(1) - y(-1)) - (y(2) - y(-2))
            dx = jnp.concatenate([dx[8 * h : 8 * h + 8] for h in range(halves)], 1)
            dy = jnp.concatenate([dy[8 * h : 8 * h + 8] for h in range(halves)], 1)
            dz = jnp.concatenate([depth_slope(comp, plane, h) for h in range(halves)], 1)
            slopes += [dx, dy, dz]
        products = [slopes[a] * slopes[9 + b] for a in range(9) for b in range(9)]
        products.append(jnp.zeros_like(products[0]))
        high, low = split(jnp.concatenate(products, 0))
        rest = jnp.zeros((DEPTH - 3 * GROUP, high.shape[1]), BF16)
        block = dot(wk_ref[...], jnp.concatenate([high, low, high, rest], 0))
        high, low = split(block)
        sh_ref[plane] = high
        sl_ref[plane] = low
        part = dot_nt(jnp.concatenate([high, low], 0), high)
        total = part if total is None else total + part

    n = total.shape[1]
    same = (iota((n, n), 0) & 7) == (iota((n, n), 1) & 7)
    main = jnp.where(same, total[:n] + total[n:], 0.0)
    cross = jnp.where(same, total[n:], 0.0).astype(BF16)
    snaps = n // 8
    et = jnp.where(
        lax.shift_right_logical(iota((snaps, n), 1), 3) == iota((snaps, n), 0), 1.0, 0.0
    )
    narrow = jnp.dot(et, main, precision=lax.Precision.HIGHEST, preferred_element_type=F32)
    narrow = narrow + dot_nt(et.astype(BF16), cross)
    tiled = jnp.where(
        lax.shift_right_logical(iota((n, 128), 0), 3) == (iota((n, 128), 1) & 31), 1.0, 0.0
    )
    gram = jnp.dot(narrow, tiled, precision=lax.Precision.HIGHEST, preferred_element_type=F32)
    packed = gram[0:8]
    for k in range(1, snaps // 8):
        packed = jnp.where(lane >= 32 * k, gram[8 * k : 8 * k + 8], packed)
    g_ref[...] = jnp.broadcast_to(packed[None], g_ref.shape)


def inverse_factor(gram, snaps):
    row, lane = iota(gram.shape, 0), iota(gram.shape, 1)
    work = jnp.where(lane < snaps, gram, jnp.where(lane == row + snaps, 1.0, 0.0))
    for k in range(snaps - 1):
        pivot = work[k : k + 1, k : k + 1]
        scaled = work[k : k + 1, :] * (1.0 / pivot)
        work = jnp.where(row > k, work - work[:, k : k + 1] * scaled, work)
    diagonal = jnp.sum(jnp.where(lane == row, work, 0.0), axis=1, keepdims=True)
    work = work * (1.0 / jnp.sqrt(diagonal))
    return jnp.where(lane < snaps, pltpu.roll(work, 128 - snaps, 1), 0.0)


def basis_kernel(cells, r_ref, sh_ref, sl_ref, o_ref, lk_ref):
    n = sh_ref.shape[1]
    snaps = n // 8

    @pl.when(pl.program_id(0) == 0)
    def _():
        packed = r_ref[0]
        for i in range(1, r_ref.shape[0]):
            packed = packed + r_ref[i]
        packed = packed * (1.0 / cells)
        gram = jnp.concatenate(
            [packed] + [pltpu.roll(packed, 128 - 32 * k, 1) for k in range(1, snaps // 8)], 0
        )
        high, low = split(inverse_factor(gram, snaps))
        to_wide = jnp.where(
            lax.shift_right_logical(iota((128, n), 1), 3) == iota((128, n), 0), 1.0, 0.0
        ).astype(BF16)
        high = spread(dot(high, to_wide).astype(BF16))
        low = spread(dot(low, to_wide).astype(BF16))
        lk_ref[:, 0:n] = high
        lk_ref[:, n : 2 * n] = high
        lk_ref[:, 2 * n : 3 * n] = low

    for plane in range(sh_ref.shape[0]):
        high = sh_ref[plane]
        out = dot(lk_ref[...], jnp.concatenate([high, sl_ref[plane], high], 0))
        for half in range(o_ref.shape[2] // 8):
            part = out[:, 128 * half : 128 * half + 128]
            o_ref[:, plane, 8 * half : 8 * half + 8, :] = part.reshape(snaps, 8, 128)


def shape(*dims, dtype=F32):
    return jax.ShapeDtypeStruct(dims, dtype)


def body(forward_velocity, adjoint_velocity, weights):
    _, planes, rows, cols = forward_velocity.shape
    snaps = weights.shape[0]
    n = 8 * snaps
    width = rows // 8 * cols
    zrows = -(-6 * planes * (rows // 8) * 4 // 128) * 8
    params = pltpu.CompilerParams(vmem_limit_bytes=48 * 2**20)

    xf, xl, yf, yl, zs = pl.pallas_call(
        sends_kernel,
        in_specs=[VMEM] * 2,
        out_specs=[VMEM] * 5,
        out_shape=[
            shape(6, 2, rows, cols),
            shape(6, 2, rows, cols),
            shape(6, planes, 2, cols),
            shape(6, planes, 2, cols),
            shape(zrows, 128),
        ],
        compiler_params=params,
        interpret=INTERPRET,
    )(forward_velocity, adjoint_velocity)

    def move(value, axis, step):
        size = lax.axis_size(axis)
        return lax.ppermute(value, axis, [(i, (i + step) % size) for i in range(size)])

    xb, xa = move(xl, "stream", 1), move(xf, "stream", -1)
    yb, ya = move(yl, "span", 1), move(yf, "span", -1)
    zb, za = move(zs, "depth", 1), move(zs, "depth", -1)

    wk = pl.pallas_call(
        weights_kernel,
        in_specs=[VMEM],
        out_specs=VMEM,
        out_shape=shape(n, DEPTH, dtype=BF16),
        compiler_params=params,
        interpret=INTERPRET,
    )(weights)

    span = lax.axis_size("span")
    others = lax.axis_size(("stream", "depth"))
    sh, sl, grams = pl.pallas_call(
        compute_kernel,
        in_specs=[VMEM] * 9,
        out_specs=[VMEM] * 3,
        out_shape=[
            shape(planes, n, width, dtype=BF16),
            shape(planes, n, width, dtype=BF16),
            shape(span, 8, 128),
        ],
        scratch_shapes=[pltpu.VMEM((6, planes, rows + 16, cols), F32)],
        compiler_params=params,
        interpret=INTERPRET,
    )(forward_velocity, adjoint_velocity, xb, xa, yb, ya, zb, za, wk)

    grams = lax.all_to_all(grams, "span", 0, 0, tiled=True)
    grams = jnp.broadcast_to(grams.sum(0)[None], (others, 8, 128))
    grams = lax.all_to_all(grams, ("stream", "depth"), 0, 0, tiled=True)

    cells = planes * rows * cols * span * others
    step = 2
    return pl.pallas_call(
        functools.partial(basis_kernel, cells),
        grid=(planes // step,),
        in_specs=[
            VMEM,
            pl.BlockSpec((step, n, width), lambda i: (i, 0, 0)),
            pl.BlockSpec((step, n, width), lambda i: (i, 0, 0)),
        ],
        out_specs=pl.BlockSpec((snaps, step, rows, cols), lambda i: (0, i, 0, 0)),
        out_shape=shape(snaps, planes, rows, cols),
        scratch_shapes=[pltpu.VMEM((n, 3 * n), BF16)],
        compiler_params=params,
        interpret=INTERPRET,
    )(grams, sh, sl)


def solution(mesh):
    spec = P(None, "stream", "span", "depth")
    return jax.shard_map(body, mesh=mesh, in_specs=(spec, spec, P()), out_specs=spec, check_vma=False)
```

time: 185 us -> 74.3 us (0.40)
  the two profiles are of different devices: /device:TPU:6 before, /device:TPU:1 now
where the time goes in v1:
time: 74.3 us; the launch traced here: 74 us
  blocking collectives  34.2 us (46%)
  starting transfers between devices  22.3 us (30%)
  Pallas kernels  10.9 us (15%)
  local copies, waits for them, and re-layouts  3.5 us (5%)
  waiting for transfers between devices  3.05 us (4%)
    ppermute x6, starting transfers between devices, move(): lax.ppermute(value, axis, [(i, (i + step) % size) for i in range(size)])  22.3 us
    all_to_all x1, blocking collectives, body(): grams = lax.all_to_all(grams, 'span', 0, 0, tiled=True)  18.5 us
    all_to_all x1, blocking collectives, body(): grams = lax.all_to_all(grams, ('stream', 'depth'), 0, 0, tiled=True)  15.6 us
    pallas_call x1, Pallas kernels, body(): pl.pallas_call(functools.partial(basis_kernel, cells), grid=(planes // st...  5.77 us
    pallas_call x1, Pallas kernels, body(): pl.pallas_call(compute_kernel, in_specs=[VMEM] * 9, out_specs=[VMEM] * 3,...  4.34 us
    unnamed x8, local copies, waits for them, and re-layouts  3.49 us
    ppermute x6, waiting for transfers between devices, move(): lax.ppermute(value, axis, [(i, (i + step) % size) for i in range(size)])  3.05 us
  transfers between devices with their start and end apart: 6, of which 2 were waited for; matrix products, arithmetic and copies ran while one was open for 0% of the time, Pallas kernels for 1%

profile of v1, /device:TPU:1, one launch (start us, length us, event | category | flops | bytes accessed | tf_op | source)
XLA Modules:
  0.0 74.0 jit_solution(15793287470598569722)
XLA Ops:
  0.0 0.0 copy-start
  0.0 0.9 %copy-done = f32[3,8,16,128]{3,2,1,0:T(8,128)S(1)} copy-done((f32[3,8,16,128]{3,2,1,0:T(8,128)S(1)}, f32[3,8,16,128]{3,2,1,0:T(8,128)}, u32[]{:S(2)}) %copy-start) | copy-done | bytes 196632
  0.9 0.0 copy-start.2
  0.9 0.9 %copy-done.2 = f32[3,8,16,128]{3,2,1,0:T(8,128)S(1)} copy-done((f32[3,8,16,128]{3,2,1,0:T(8,128)S(1)}, f32[3,8,16,128]{3,2,1,0:T(8,128)}, u32[]{:S(2)}) %copy-start.2) | copy-done | bytes 196632
  1.9 0.2 shard_map.37
  2.0 4.8 %collective-permute-start = (f32[6,2,16,128]{3,2,1,0:T(8,128)S(1)}, f32[6,2,16,128]{3,2,1,0:T(8,128)S(1)}, u32[]{:S(2)}, u32[]{:S(2)}) collective-permute-start(f32[6,2,16,128]{3,2,1,0:T(8,128)S(1)} %get-tuple-element.13), channel_id=1, source_target_pairs={{0,64},{64,128},{128,192},{192,256},{256,320},{320,384},{384,448},... | collective-permute-start | bytes 294920 | tf_op jit(solution)/shard_map/ppermute | solution.py:231
  6.9 8.6 %collective-permute-start.1 = (f32[6,2,16,128]{3,2,1,0:T(8,128)S(1)}, f32[6,2,16,128]{3,2,1,0:T(8,128)S(1)}, u32[]{:S(2)}, u32[]{:S(2)}) collective-permute-start(f32[6,2,16,128]{3,2,1,0:T(8,128)S(1)} %get-tuple-element.14), channel_id=1, source_target_pairs={{0,448},{64,0},{128,64},{192,128},{256,192},{320,256},{384,320},{4... | collective-permute-start | bytes 294920 | tf_op jit(solution)/shard_map/ppermute | solution.py:231
  15.5 2.1 %collective-permute-start.2 = (f32[6,8,2,128]{3,2,1,0:T(2,128)S(1)}, f32[6,8,2,128]{3,2,1,0:T(2,128)S(1)}, u32[]{:S(2)}, u32[]{:S(2)}) collective-permute-start(f32[6,8,2,128]{3,2,1,0:T(2,128)S(1)} %get-tuple-element.15), channel_id=1, source_target_pairs={{0,4},{4,8},{8,12},{12,16},{16,20},{20,24},{24,28},{28,32},{32,36}... | collective-permute-start | bytes 147464 | tf_op jit(solution)/shard_map/ppermute | solution.py:231
  17.6 0.0 collective-permute-start.3
  17.6 4.4 %collective-permute-start.5 = (f32[24,128]{1,0:T(8,128)S(1)}, f32[24,128]{1,0:T(8,128)S(1)}, u32[]{:S(2)}, u32[]{:S(2)}) collective-permute-start(f32[24,128]{1,0:T(8,128)S(1)} %get-tuple-element.17), channel_id=1, source_target_pairs={{0,3},{1,0},{2,1},{3,2},{4,7},{5,4},{6,5},{7,6},{8,11},{9,8},{10,9... | collective-permute-start | bytes 36872 | tf_op jit(solution)/shard_map/ppermute | solution.py:231
  22.0 0.8 %collective-permute-done.5.za = f32[24,128]{1,0:T(8,128)S(1)} collective-permute-done((f32[24,128]{1,0:T(8,128)S(1)}, f32[24,128]{1,0:T(8,128)S(1)}, u32[]{:S(2)}, u32[]{:S(2)}) %collective-permute-start.5) | collective-permute-done | bytes 12320 | tf_op jit(solution)/shard_map/ppermute | solution.py:231
  22.8 2.3 %collective-permute-start.4 = (f32[24,128]{1,0:T(8,128)S(1)}, f32[24,128]{1,0:T(8,128)S(1)}, u32[]{:S(2)}, u32[]{:S(2)}) collective-permute-start(f32[24,128]{1,0:T(8,128)S(1)} %get-tuple-element.17), channel_id=1, source_target_pairs={{0,1},{1,2},{2,3},{3,0},{4,5},{5,6},{6,7},{7,4},{8,9},{9,10},{10,1... | collective-permute-start | bytes 36872 | tf_op jit(solution)/shard_map/ppermute | solution.py:231
  25.1 0.0 copy-start.3
  25.2 0.7 copy-done.3
  25.9 0.6 shard_map.38.wk_ref
  26.5 2.2 %collective-permute-done.4.zb = f32[24,128]{1,0:T(8,128)S(1)} collective-permute-done((f32[24,128]{1,0:T(8,128)S(1)}, f32[24,128]{1,0:T(8,128)S(1)}, u32[]{:S(2)}, u32[]{:S(2)}) %collective-permute-start.4) | collective-permute-done | bytes 12320 | tf_op jit(solution)/shard_map/ppermute | solution.py:231
  28.7 0.0 collective-permute-done.2.yb
  28.7 0.0 collective-permute-done.3.ya
  28.7 0.0 collective-permute-done.xb
  28.7 0.0 collective-permute-done.1.xa
  28.7 0.0 copy-start.1
  28.7 0.9 %copy-done.1 = f32[3,8,16,128]{3,2,1,0:T(8,128)S(1)} copy-done((f32[3,8,16,128]{3,2,1,0:T(8,128)S(1)}, f32[3,8,16,128]{3,2,1,0:T(8,128)}, u32[]{:S(2)}) %copy-start.1) | copy-done | bytes 196632
  29.7 4.3 %shard_map.39 = (bf16[8,256,256]{2,1,0:T(8,128)(2,1)S(1)}, bf16[8,256,256]{2,1,0:T(8,128)(2,1)S(1)}, f32[16,8,128]{2,1,0:T(8,128)S(1)}) custom-call(f32[3,8,16,128]{3,2,1,0:T(8,128)S(1)} %copy-done.1, f32[3,8,16,128]{3,2,1,0:T(8,128)S(1)} %copy-done.2, f32[6,2,16,128]{3,2,1,0:T(8,128)S(1)} %collective-permute-done.xb, ...), custom_call_target="tpu_custom_call" | custom-call | tf_op jit(solution)/shard_map/pallas_call | solution.py:248
  34.0 18.5 %all_to_all.10 = f32[16,8,128]{2,1,0:T(8,128)S(1)} all-to-all(f32[16,8,128]{2,1,0:T(8,128)S(1)} %get-tuple-element.18), channel_id=1, replica_groups=mesh['stream'=8,'span'=16,'depth'=4] {'span'}, dimensions={0} | all-to-all | bytes 131072 | tf_op jit(solution)/shard_map/all_to_all | solution.py:262
  52.5 15.6 %all_to_all.11.r_ref = f32[32,8,128]{2,1,0:T(8,128)S(1)} all-to-all(f32[32,8,128]{2,1,0:T(8,128)S(1)} %broadcast_in_dim.2), channel_id=1, replica_groups=mesh['stream'=8,'span'=16,'depth'=4] {'stream','depth'}, dimensions={0} | all-to-all | bytes 262144 | tf_op jit(solution)/shard_map/all_to_all | solution.py:264
  68.2 5.8 %shard_map.40 = f32[32,8,16,128]{3,2,1,0:T(8,128)} custom-call(f32[32,8,128]{2,1,0:T(8,128)S(1)} %all_to_all.11.r_ref, bf16[8,256,256]{2,1,0:T(8,128)(2,1)S(1)} %get-tuple-element.19.sh_ref, bf16[8,256,256]{2,1,0:T(8,128)(2,1)S(1)} %get-tuple-element.20.sl_ref), custom_call_target="tpu_custom_call" | custom-call | tf_op jit(solution)/shard_map/pallas_call | solution.py:268
  (2 shorter events, 0.0 us)
Async XLA Ops:
  0.0 0.9 %copy-start = (f32[3,8,16,128]{3,2,1,0:T(8,128)S(1)}, f32[3,8,16,128]{3,2,1,0:T(8,128)}, u32[]{:S(2)}) copy-start(f32[3,8,16,128]{3,2,1,0:T(8,128)} %f_ref.3) | copy-start | bytes 589828
  0.9 0.9 %copy-start.2 = (f32[3,8,16,128]{3,2,1,0:T(8,128)S(1)}, f32[3,8,16,128]{3,2,1,0:T(8,128)}, u32[]{:S(2)}) copy-start(f32[3,8,16,128]{3,2,1,0:T(8,128)} %a_ref.3) | copy-start | bytes 589828
  2.0 26.7 %collective-permute-start = (f32[6,2,16,128]{3,2,1,0:T(8,128)S(1)}, f32[6,2,16,128]{3,2,1,0:T(8,128)S(1)}, u32[]{:S(2)}, u32[]{:S(2)}) collective-permute-start(f32[6,2,16,128]{3,2,1,0:T(8,128)S(1)} %get-tuple-element.13), channel_id=1, source_target_pairs={{0,64},{64,128},{128,192},{192,256},{256,320},{320,384},{384,448},... | collective-permute-start | bytes 294920 | tf_op jit(solution)/shard_map/ppermute | solution.py:231
  6.9 21.9 %collective-permute-start.1 = (f32[6,2,16,128]{3,2,1,0:T(8,128)S(1)}, f32[6,2,16,128]{3,2,1,0:T(8,128)S(1)}, u32[]{:S(2)}, u32[]{:S(2)}) collective-permute-start(f32[6,2,16,128]{3,2,1,0:T(8,128)S(1)} %get-tuple-element.14), channel_id=1, source_target_pairs={{0,448},{64,0},{128,64},{192,128},{256,192},{320,256},{384,320},{4... | collective-permute-start | bytes 294920 | tf_op jit(solution)/shard_map/ppermute | solution.py:231
  15.5 13.2 %collective-permute-start.2 = (f32[6,8,2,128]{3,2,1,0:T(2,128)S(1)}, f32[6,8,2,128]{3,2,1,0:T(2,128)S(1)}, u32[]{:S(2)}, u32[]{:S(2)}) collective-permute-start(f32[6,8,2,128]{3,2,1,0:T(2,128)S(1)} %get-tuple-element.15), channel_id=1, source_target_pairs={{0,4},{4,8},{8,12},{12,16},{16,20},{20,24},{24,28},{28,32},{32,36}... | collective-permute-start | bytes 147464 | tf_op jit(solution)/shard_map/ppermute | solution.py:231
  17.6 11.1 %collective-permute-start.3 = (f32[6,8,2,128]{3,2,1,0:T(2,128)S(1)}, f32[6,8,2,128]{3,2,1,0:T(2,128)S(1)}, u32[]{:S(2)}, u32[]{:S(2)}) collective-permute-start(f32[6,8,2,128]{3,2,1,0:T(2,128)S(1)} %get-tuple-element.16), channel_id=1, source_target_pairs={{0,60},{4,0},{8,4},{12,8},{16,12},{20,16},{24,20},{28,24},{32,28},... | collective-permute-start | bytes 147464 | tf_op jit(solution)/shard_map/ppermute | solution.py:231
  17.6 5.2 %collective-permute-start.5 = (f32[24,128]{1,0:T(8,128)S(1)}, f32[24,128]{1,0:T(8,128)S(1)}, u32[]{:S(2)}, u32[]{:S(2)}) collective-permute-start(f32[24,128]{1,0:T(8,128)S(1)} %get-tuple-element.17), channel_id=1, source_target_pairs={{0,3},{1,0},{2,1},{3,2},{4,7},{5,4},{6,5},{7,6},{8,11},{9,8},{10,9... | collective-permute-start | bytes 36872 | tf_op jit(solution)/shard_map/ppermute | solution.py:231
  22.8 5.9 %collective-permute-start.4 = (f32[24,128]{1,0:T(8,128)S(1)}, f32[24,128]{1,0:T(8,128)S(1)}, u32[]{:S(2)}, u32[]{:S(2)}) collective-permute-start(f32[24,128]{1,0:T(8,128)S(1)} %get-tuple-element.17), channel_id=1, source_target_pairs={{0,1},{1,2},{2,3},{3,0},{4,5},{5,6},{6,7},{7,4},{8,9},{9,10},{10,1... | collective-permute-start | bytes 36872 | tf_op jit(solution)/shard_map/ppermute | solution.py:231
  25.1 0.7 copy-start.3
  28.7 0.9 %copy-start.1 = (f32[3,8,16,128]{3,2,1,0:T(8,128)S(1)}, f32[3,8,16,128]{3,2,1,0:T(8,128)}, u32[]{:S(2)}) copy-start(f32[3,8,16,128]{3,2,1,0:T(8,128)} %f_ref.3) | copy-start | bytes 589828

commit v2 on v1

--- a/solution.py
+++ b/solution.py
@@ -11,8 +11,10 @@
 BF16 = jnp.bfloat16
 INTERPRET = False
 VMEM = pl.BlockSpec(memory_space=pltpu.VMEM)
+HBM = pl.BlockSpec(memory_space=pltpu.HBM)
 GROUP = 82 * 8
 DEPTH = 2048
+BLOCK = 8
 
 
 def iota(shape, dim):
@@ -37,22 +39,28 @@
     return divmod(index * 4, 128)
 
 
-def sends_kernel(f_ref, a_ref, xf, xl, yf, yl, zs):
-    planes, rows = f_ref.shape[1], f_ref.shape[2]
-    for ref, base in ((f_ref, 0), (a_ref, 3)):
-        part = slice(base, base + 3)
-        xf[part] = ref[:, 0:2]
-        xl[part] = ref[:, planes - 2 : planes]
-        yf[part] = ref[:, :, 0:2, :]
-        yl[part] = ref[:, :, rows - 2 : rows, :]
+def sends_kernel(f_hbm, a_hbm, w_hbm, fields, w_ref, xf, xl, yf, yl, zs, sems):
+    copies = [
+        pltpu.make_async_copy(f_hbm, fields.at[0:3], sems.at[0]),
+        pltpu.make_async_copy(a_hbm, fields.at[3:6], sems.at[1]),
+        pltpu.make_async_copy(w_hbm, w_ref, sems.at[2]),
+    ]
+    for copy in copies:
+        copy.start()
+    for copy in copies:
+        copy.wait()
+    comps, planes, rows = fields.shape[:3]
+    xf[...] = fields[:, 0:2]
+    xl[...] = fields[:, planes - 2 : planes]
+    yf[...] = fields[:, :, 0:2, :]
+    yl[...] = fields[:, :, rows - 2 : rows, :]
     lane = iota((8, 128), 1)
     packed = [jnp.zeros((8, 128), F32) for _ in range(zs.shape[0] // 8)]
-    for comp in range(6):
-        ref = f_ref if comp < 3 else a_ref
+    for comp in range(comps):
         for plane in range(planes):
             for half in range(rows // 8):
                 group, at = place((comp * planes + plane) * (rows // 8) + half)
-                tile = ref[comp % 3, plane, 8 * half : 8 * half + 8, :]
+                tile = fields[comp, plane, 8 * half : 8 * half + 8, :]
                 moved = pltpu.roll(tile, (2 + at) % 128, 1)
                 here = (lane >= at) & (lane < at + 4)
                 packed[group] = jnp.where(here, moved, packed[group])
@@ -83,15 +91,12 @@
     return jnp.where(same, tall, 0.0).astype(BF16)
 
 
-def compute_kernel(f_ref, a_ref, xb, xa, yb, ya, zb, za, wk_ref, sh_ref, sl_ref, g_ref, ypad):
-    planes, rows = f_ref.shape[1], f_ref.shape[2]
+def compute_kernel(fields, xb, xa, yb, ya, zb, za, wk_ref, sh_ref, sl_ref, g_ref, ypad):
+    planes, rows = fields.shape[1], fields.shape[2]
     halves = rows // 8
     lane = iota((8, 128), 1)
     total = None
-    for comp in range(6):
-        ref = f_ref if comp < 3 else a_ref
-        for plane in range(planes):
-            ypad[comp, plane, 8 : 8 + rows, :] = ref[comp % 3, plane]
+    ypad[:, :, 8 : 8 + rows, :] = fields[...]
     ypad[:, :, 6:8, :] = yb[...]
     ypad[:, :, 8 + rows : 10 + rows, :] = ya[...]
 
@@ -100,10 +105,10 @@
             return xb[comp, plane + 2]
         if plane >= planes:
             return xa[comp, plane - planes]
-        return (f_ref if comp < 3 else a_ref)[comp % 3, plane]
+        return fields[comp, plane]
 
     def depth_slope(comp, plane, half):
-        tile = ypad[comp, plane, 8 + 8 * half : 16 + 8 * half, :]
+        tile = fields[comp, plane, 8 * half : 8 * half + 8, :]
         group, at = place((comp * planes + plane) * halves + half)
         before = zb[8 * group : 8 * group + 8, :]
         after = za[8 * group : 8 * group + 8, :]
@@ -159,44 +164,56 @@
 def inverse_factor(gram, snaps):
     row, lane = iota(gram.shape, 0), iota(gram.shape, 1)
     work = jnp.where(lane < snaps, gram, jnp.where(lane == row + snaps, 1.0, 0.0))
-    for k in range(snaps - 1):
-        pivot = work[k : k + 1, k : k + 1]
-        scaled = work[k : k + 1, :] * (1.0 / pivot)
-        work = jnp.where(row > k, work - work[:, k : k + 1] * scaled, work)
+    for first in range(0, snaps, BLOCK):
+        block = range(first, first + BLOCK)
+        cols = [jnp.broadcast_to(work[:, k : k + 1], work.shape) for k in block]
+        rows = [work[k : k + 1, :] for k in block]
+        for i, k in enumerate(block):
+            inverse = 1.0 / cols[i][k : k + 1, :]
+            below = jnp.where(row > k, cols[i], 0.0)
+            scaled = rows[i] * inverse
+            work = work - below * scaled
+            for j in range(i + 1, BLOCK):
+                entry = cols[i][first + j : first + j + 1, :]
+                cols[j] = cols[j] - below * (entry * inverse)
+                rows[j] = rows[j] - entry * scaled
     diagonal = jnp.sum(jnp.where(lane == row, work, 0.0), axis=1, keepdims=True)
     work = work * (1.0 / jnp.sqrt(diagonal))
     return jnp.where(lane < snaps, pltpu.roll(work, 128 - snaps, 1), 0.0)
 
 
-def basis_kernel(cells, r_ref, sh_ref, sl_ref, o_ref, lk_ref):
-    n = sh_ref.shape[1]
+def basis_kernel(cells, r_ref, sh_ref, sl_ref, o_hbm, lk_ref, out_ref, sems):
+    planes, n = sh_ref.shape[:2]
     snaps = n // 8
-
-    @pl.when(pl.program_id(0) == 0)
-    def _():
-        packed = r_ref[0]
-        for i in range(1, r_ref.shape[0]):
-            packed = packed + r_ref[i]
-        packed = packed * (1.0 / cells)
-        gram = jnp.concatenate(
-            [packed] + [pltpu.roll(packed, 128 - 32 * k, 1) for k in range(1, snaps // 8)], 0
-        )
-        high, low = split(inverse_factor(gram, snaps))
-        to_wide = jnp.where(
-            lax.shift_right_logical(iota((128, n), 1), 3) == iota((128, n), 0), 1.0, 0.0
-        ).astype(BF16)
-        high = spread(dot(high, to_wide).astype(BF16))
-        low = spread(dot(low, to_wide).astype(BF16))
-        lk_ref[:, 0:n] = high
-        lk_ref[:, n : 2 * n] = high
-        lk_ref[:, 2 * n : 3 * n] = low
-
-    for plane in range(sh_ref.shape[0]):
+    packed = r_ref[0]
+    for i in range(1, r_ref.shape[0]):
+        packed = packed + r_ref[i]
+    packed = packed * (1.0 / cells)
+    gram = jnp.concatenate(
+        [packed] + [pltpu.roll(packed, 128 - 32 * k, 1) for k in range(1, snaps // 8)], 0
+    )
+    high, low = split(inverse_factor(gram, snaps))
+    to_wide = jnp.where(
+        lax.shift_right_logical(iota((128, n), 1), 3) == iota((128, n), 0), 1.0, 0.0
+    ).astype(BF16)
+    high = spread(dot(high, to_wide).astype(BF16))
+    low = spread(dot(low, to_wide).astype(BF16))
+    lk_ref[:, 0:n] = high
+    lk_ref[:, n : 2 * n] = high
+    lk_ref[:, 2 * n : 3 * n] = low
+
+    copies = []
+    for plane in range(planes):
         high = sh_ref[plane]
         out = dot(lk_ref[...], jnp.concatenate([high, sl_ref[plane], high], 0))
-        for half in range(o_ref.shape[2] // 8):
+        for half in range(out_ref.shape[2] // 8):
             part = out[:, 128 * half : 128 * half + 128]
-            o_ref[:, plane, 8 * half : 8 * half + 8, :] = part.reshape(snaps, 8, 128)
+            out_ref[plane, :, 8 * half : 8 * half + 8, :] = part.reshape(snaps, 8, 128)
+        copy = pltpu.make_async_copy(out_ref.at[plane], o_hbm.at[:, plane], sems.at[plane])
+        copy.start()
+        copies.append(copy)
+    for copy in copies:
+        copy.wait()
 
 
 def shape(*dims, dtype=F32):
@@ -211,20 +228,23 @@
     zrows = -(-6 * planes * (rows // 8) * 4 // 128) * 8
     params = pltpu.CompilerParams(vmem_limit_bytes=48 * 2**20)
 
-    xf, xl, yf, yl, zs = pl.pallas_call(
+    fields, w, xf, xl, yf, yl, zs = pl.pallas_call(
         sends_kernel,
-        in_specs=[VMEM] * 2,
-        out_specs=[VMEM] * 5,
+        in_specs=[HBM] * 3,
+        out_specs=[VMEM] * 7,
         out_shape=[
+            shape(6, planes, rows, cols),
+            shape(*weights.shape),
             shape(6, 2, rows, cols),
             shape(6, 2, rows, cols),
             shape(6, planes, 2, cols),
             shape(6, planes, 2, cols),
             shape(zrows, 128),
         ],
+        scratch_shapes=[pltpu.SemaphoreType.DMA((3,))],
         compiler_params=params,
         interpret=INTERPRET,
-    )(forward_velocity, adjoint_velocity)
+    )(*(pltpu.with_memory_space_constraint(x, pltpu.HBM) for x in (forward_velocity, adjoint_velocity, weights)))
 
     def move(value, axis, step):
         size = lax.axis_size(axis)
@@ -232,7 +252,8 @@
 
     xb, xa = move(xl, "stream", 1), move(xf, "stream", -1)
     yb, ya = move(yl, "span", 1), move(yf, "span", -1)
-    zb, za = move(zs, "depth", 1), move(zs, "depth", -1)
+    zb = move(lax.optimization_barrier((zs, xb))[0], "depth", 1)
+    za = move(lax.optimization_barrier((zs, xa))[0], "depth", -1)
 
     wk = pl.pallas_call(
         weights_kernel,
@@ -241,13 +262,13 @@
         out_shape=shape(n, DEPTH, dtype=BF16),
         compiler_params=params,
         interpret=INTERPRET,
-    )(weights)
+    )(w)
 
     span = lax.axis_size("span")
     others = lax.axis_size(("stream", "depth"))
     sh, sl, grams = pl.pallas_call(
         compute_kernel,
-        in_specs=[VMEM] * 9,
+        in_specs=[VMEM] * 8,
         out_specs=[VMEM] * 3,
         out_shape=[
             shape(planes, n, width, dtype=BF16),
@@ -257,25 +278,23 @@
         scratch_shapes=[pltpu.VMEM((6, planes, rows + 16, cols), F32)],
         compiler_params=params,
         interpret=INTERPRET,
-    )(forward_velocity, adjoint_velocity, xb, xa, yb, ya, zb, za, wk)
+    )(fields, xb, xa, yb, ya, zb, za, wk)
 
     grams = lax.all_to_all(grams, "span", 0, 0, tiled=True)
     grams = jnp.broadcast_to(grams.sum(0)[None], (others, 8, 128))
     grams = lax.all_to_all(grams, ("stream", "depth"), 0, 0, tiled=True)
 
     cells = planes * rows * cols * span * others
-    step = 2
     return pl.pallas_call(
         functools.partial(basis_kernel, cells),
-        grid=(planes // step,),
-        in_specs=[
-            VMEM,
-            pl.BlockSpec((step, n, width), lambda i: (i, 0, 0)),
-            pl.BlockSpec((step, n, width), lambda i: (i, 0, 0)),
+        in_specs=[VMEM] * 3,
+        out_specs=HBM,
+        out_shape=shape(snaps, planes, rows, cols),
+        scratch_shapes=[
+            pltpu.VMEM((n, 3 * n), BF16),
+            pltpu.VMEM((planes, snaps, rows, cols), F32),
+            pltpu.SemaphoreType.DMA((planes,)),
         ],
-        out_specs=pl.BlockSpec((snaps, step, rows, cols), lambda i: (0, i, 0, 0)),
-        out_shape=shape(snaps, planes, rows, cols),
-        scratch_shapes=[pltpu.VMEM((n, 3 * n), BF16)],
         compiler_params=params,
         interpret=INTERPRET,
     )(grams, sh, sl)

time: 74.3 us -> 66.7 us (0.90)
  local copies, waits for them, and re-layouts: 3.5 us -> 0.01 us
  waiting for transfers between devices: 3.05 us -> 0.74 us
  Pallas kernels: 10.9 us -> 9.29 us
    unnamed x8 -> x0, local copies, waits for them, and re-layouts: 3.49 us -> none
    ppermute x6, waiting for transfers between devices: 3.05 us -> 0.74 us  [move(): lax.ppermute(value, axis, [(i, (i + step) % size) for i in range(size)])]
    pallas_call x3, Pallas kernels: 10.3 us -> 8.7 us  [the longest x1 4.44 us: body(): pl.pallas_call(compute_kernel, in_specs=[VMEM] * 8, out_specs=[VMEM] * 3,...]
    all_to_all x1, blocking collectives: 15.6 us -> 16.6 us  [body(): grams = lax.all_to_all(grams, ('stream', 'depth'), 0, 0, tiled=True)]
    all_to_all x1, blocking collectives: 18.5 us -> 17.6 us  [body(): grams = lax.all_to_all(grams, 'span', 0, 0, tiled=True)]
  transfers between devices with their start and end apart: 6 -> 6, of which waited for: 2 -> 1; matrix products, arithmetic and copies ran while one was open for 0% -> 0% of each run, Pallas kernels for 1% -> 1%
where the time goes in v2:
time: 66.7 us; the launch traced here: 66.4 us
  blocking collectives  34.2 us (51%)
  starting transfers between devices  22.1 us (33%)
  Pallas kernels  9.29 us (14%)
  waiting for transfers between devices  0.74 us (1%)
    ppermute x6, starting transfers between devices, move(): lax.ppermute(value, axis, [(i, (i + step) % size) for i in range(size)])  22.1 us
    all_to_all x1, blocking collectives, body(): grams = lax.all_to_all(grams, 'span', 0, 0, tiled=True)  17.6 us
    all_to_all x1, blocking collectives, body(): grams = lax.all_to_all(grams, ('stream', 'depth'), 0, 0, tiled=True)  16.6 us
    pallas_call x1, Pallas kernels, body(): pl.pallas_call(compute_kernel, in_specs=[VMEM] * 8, out_specs=[VMEM] * 3,...  4.44 us
    pallas_call x1, Pallas kernels, body(): pl.pallas_call(functools.partial(basis_kernel, cells), in_specs=[VMEM] *...  3.01 us
  transfers between devices with their start and end apart: 6, of which 1 were waited for; matrix products, arithmetic and copies ran while one was open for 0% of the time, Pallas kernels for 1%

profile of v2, /device:TPU:1, one launch (start us, length us, event | category | flops | bytes accessed | tf_op | source)
XLA Modules:
  0.0 66.4 jit_solution(1725666584860499930)
XLA Ops:
  0.0 1.3 %shard_map.37 = (f32[6,8,16,128]{3,2,1,0:T(8,128)S(1)}, f32[32,81]{1,0:T(8,128)S(1)}, f32[6,2,16,128]{3,2,1,0:T(8,128)S(1)}, f32[6,2,16,128]{3,2,1,0:T(8,128)S(1...) custom-call(f32[3,8,16,128]{3,2,1,0:T(8,128)} %f_hbm.1, ...), custom_call_target="tpu_custom_call" | custom-call | tf_op jit(solution)/shard_map/pallas_call | solution.py:231
  1.3 4.8 %collective-permute-start = (f32[6,2,16,128]{3,2,1,0:T(8,128)S(1)}, f32[6,2,16,128]{3,2,1,0:T(8,128)S(1)}, u32[]{:S(2)}, u32[]{:S(2)}) collective-permute-start(f32[6,2,16,128]{3,2,1,0:T(8,128)S(1)} %get-tuple-element.18), channel_id=1, source_target_pairs={{0,64},{64,128},{128,192},{192,256},{256,320},{320,384},{384,448},... | collective-permute-start | bytes 294920 | tf_op jit(solution)/shard_map/ppermute | solution.py:251
  6.1 8.6 %collective-permute-start.1 = (f32[6,2,16,128]{3,2,1,0:T(8,128)S(1)}, f32[6,2,16,128]{3,2,1,0:T(8,128)S(1)}, u32[]{:S(2)}, u32[]{:S(2)}) collective-permute-start(f32[6,2,16,128]{3,2,1,0:T(8,128)S(1)} %get-tuple-element.19), channel_id=1, source_target_pairs={{0,448},{64,0},{128,64},{192,128},{256,192},{320,256},{384,320},{4... | collective-permute-start | bytes 294920 | tf_op jit(solution)/shard_map/ppermute | solution.py:251
  14.7 2.1 %collective-permute-start.2 = (f32[6,8,2,128]{3,2,1,0:T(2,128)S(1)}, f32[6,8,2,128]{3,2,1,0:T(2,128)S(1)}, u32[]{:S(2)}, u32[]{:S(2)}) collective-permute-start(f32[6,8,2,128]{3,2,1,0:T(2,128)S(1)} %get-tuple-element.20), channel_id=1, source_target_pairs={{0,4},{4,8},{8,12},{12,16},{16,20},{20,24},{24,28},{28,32},{32,36}... | collective-permute-start | bytes 147464 | tf_op jit(solution)/shard_map/ppermute | solution.py:251
  16.8 0.0 collective-permute-start.3
  16.9 0.0 collective-permute-done.xb
  16.9 3.1 %collective-permute-start.4 = (f32[24,128]{1,0:T(8,128)S(1)}, f32[24,128]{1,0:T(8,128)S(1)}, u32[]{:S(2)}, u32[]{:S(2)}) collective-permute-start(f32[24,128]{1,0:T(8,128)S(1)} %get-tuple-element.24), channel_id=1, source_target_pairs={{0,1},{1,2},{2,3},{3,0},{4,5},{5,6},{6,7},{7,4},{8,9},{9,10},{10,1... | collective-permute-start | bytes 36872 | tf_op jit(solution)/shard_map/ppermute | solution.py:251
  20.0 0.0 collective-permute-done.1.xa
  20.0 3.4 %collective-permute-start.5 = (f32[24,128]{1,0:T(8,128)S(1)}, f32[24,128]{1,0:T(8,128)S(1)}, u32[]{:S(2)}, u32[]{:S(2)}) collective-permute-start(f32[24,128]{1,0:T(8,128)S(1)} %get-tuple-element.24), channel_id=1, source_target_pairs={{0,3},{1,0},{2,1},{3,2},{4,7},{5,4},{6,5},{7,6},{8,11},{9,8},{10,9... | collective-permute-start | bytes 36872 | tf_op jit(solution)/shard_map/ppermute | solution.py:251
  23.4 0.6 shard_map.38.wk_ref
  24.0 0.0 collective-permute-done.2.yb
  24.0 0.0 collective-permute-done.3.ya
  24.0 0.0 collective-permute-done.4.zb
  24.0 0.7 %collective-permute-done.5.za = f32[24,128]{1,0:T(8,128)S(1)} collective-permute-done((f32[24,128]{1,0:T(8,128)S(1)}, f32[24,128]{1,0:T(8,128)S(1)}, u32[]{:S(2)}, u32[]{:S(2)}) %collective-permute-start.5) | collective-permute-done | bytes 12320 | tf_op jit(solution)/shard_map/ppermute | solution.py:251
  24.7 4.4 %shard_map.39 = (bf16[8,256,256]{2,1,0:T(8,128)(2,1)S(1)}, bf16[8,256,256]{2,1,0:T(8,128)(2,1)S(1)}, f32[16,8,128]{2,1,0:T(8,128)S(1)}) custom-call(f32[6,8,16,128]{3,2,1,0:T(8,128)S(1)} %get-tuple-element.17.fields, f32[6,2,16,128]{3,2,1,0:T(8,128)S(1)} %collective-permute-done.xb, f32[6,2,16,128]{3,2,1,0:T(8,128)S(1)} %collective-permute-done.1.xa, ...), custom_call_target="tpu_custom_call" | custom-call | tf_op jit(solution)/shard_map/pallas_call | solution.py:269
  29.2 17.6 %all_to_all.10 = f32[16,8,128]{2,1,0:T(8,128)S(1)} all-to-all(f32[16,8,128]{2,1,0:T(8,128)S(1)} %get-tuple-element.26), channel_id=1, replica_groups=mesh['stream'=8,'span'=16,'depth'=4] {'span'}, dimensions={0} | all-to-all | bytes 131072 | tf_op jit(solution)/shard_map/all_to_all | solution.py:283
  46.8 16.6 %all_to_all.11.r_ref = f32[32,8,128]{2,1,0:T(8,128)S(1)} all-to-all(f32[32,8,128]{2,1,0:T(8,128)S(1)} %broadcast_in_dim.2), channel_id=1, replica_groups=mesh['stream'=8,'span'=16,'depth'=4] {'stream','depth'}, dimensions={0} | all-to-all | bytes 262144 | tf_op jit(solution)/shard_map/all_to_all | solution.py:285
  63.4 3.0 %shard_map.40 = f32[32,8,16,128]{3,2,1,0:T(8,128)} custom-call(f32[32,8,128]{2,1,0:T(8,128)S(1)} %all_to_all.11.r_ref, bf16[8,256,256]{2,1,0:T(8,128)(2,1)S(1)} %get-tuple-element.27.sh_ref, bf16[8,256,256]{2,1,0:T(8,128)(2,1)S(1)} %get-tuple-element.28.sl_ref), custom_call_target="tpu_custom_call" | custom-call | tf_op jit(solution)/shard_map/pallas_call | solution.py:288
  (2 shorter events, 0.0 us)
Async XLA Ops:
  1.3 15.6 %collective-permute-start = (f32[6,2,16,128]{3,2,1,0:T(8,128)S(1)}, f32[6,2,16,128]{3,2,1,0:T(8,128)S(1)}, u32[]{:S(2)}, u32[]{:S(2)}) collective-permute-start(f32[6,2,16,128]{3,2,1,0:T(8,128)S(1)} %get-tuple-element.18), channel_id=1, source_target_pairs={{0,64},{64,128},{128,192},{192,256},{256,320},{320,384},{384,448},... | collective-permute-start | bytes 294920 | tf_op jit(solution)/shard_map/ppermute | solution.py:251
  6.1 13.9 %collective-permute-start.1 = (f32[6,2,16,128]{3,2,1,0:T(8,128)S(1)}, f32[6,2,16,128]{3,2,1,0:T(8,128)S(1)}, u32[]{:S(2)}, u32[]{:S(2)}) collective-permute-start(f32[6,2,16,128]{3,2,1,0:T(8,128)S(1)} %get-tuple-element.19), channel_id=1, source_target_pairs={{0,448},{64,0},{128,64},{192,128},{256,192},{320,256},{384,320},{4... | collective-permute-start | bytes 294920 | tf_op jit(solution)/shard_map/ppermute | solution.py:251
  14.7 9.3 %collective-permute-start.2 = (f32[6,8,2,128]{3,2,1,0:T(2,128)S(1)}, f32[6,8,2,128]{3,2,1,0:T(2,128)S(1)}, u32[]{:S(2)}, u32[]{:S(2)}) collective-permute-start(f32[6,8,2,128]{3,2,1,0:T(2,128)S(1)} %get-tuple-element.20), channel_id=1, source_target_pairs={{0,4},{4,8},{8,12},{12,16},{16,20},{20,24},{24,28},{28,32},{32,36}... | collective-permute-start | bytes 147464 | tf_op jit(solution)/shard_map/ppermute | solution.py:251
  16.8 7.1 %collective-permute-start.3 = (f32[6,8,2,128]{3,2,1,0:T(2,128)S(1)}, f32[6,8,2,128]{3,2,1,0:T(2,128)S(1)}, u32[]{:S(2)}, u32[]{:S(2)}) collective-permute-start(f32[6,8,2,128]{3,2,1,0:T(2,128)S(1)} %get-tuple-element.21), channel_id=1, source_target_pairs={{0,60},{4,0},{8,4},{12,8},{16,12},{20,16},{24,20},{28,24},{32,28},... | collective-permute-start | bytes 147464 | tf_op jit(solution)/shard_map/ppermute | solution.py:251
  16.9 7.1 %collective-permute-start.4 = (f32[24,128]{1,0:T(8,128)S(1)}, f32[24,128]{1,0:T(8,128)S(1)}, u32[]{:S(2)}, u32[]{:S(2)}) collective-permute-start(f32[24,128]{1,0:T(8,128)S(1)} %get-tuple-element.24), channel_id=1, source_target_pairs={{0,1},{1,2},{2,3},{3,0},{4,5},{5,6},{6,7},{7,4},{8,9},{9,10},{10,1... | collective-permute-start | bytes 36872 | tf_op jit(solution)/shard_map/ppermute | solution.py:251
  20.0 4.7 %collective-permute-start.5 = (f32[24,128]{1,0:T(8,128)S(1)}, f32[24,128]{1,0:T(8,128)S(1)}, u32[]{:S(2)}, u32[]{:S(2)}) collective-permute-start(f32[24,128]{1,0:T(8,128)S(1)} %get-tuple-element.24), channel_id=1, source_target_pairs={{0,3},{1,0},{2,1},{3,2},{4,7},{5,4},{6,5},{7,6},{8,11},{9,8},{10,9... | collective-permute-start | bytes 36872 | tf_op jit(solution)/shard_map/ppermute | solution.py:251

commit v3 on v2

--- a/solution.py
+++ b/solution.py
@@ -12,8 +12,8 @@
 INTERPRET = False
 VMEM = pl.BlockSpec(memory_space=pltpu.VMEM)
 HBM = pl.BlockSpec(memory_space=pltpu.HBM)
-GROUP = 82 * 8
-DEPTH = 2048
+GROUP = 80
+DEPTH = 256
 BLOCK = 8
 
 
@@ -73,25 +73,17 @@
     high, low = split(w_ref[...] * (1.0 / 144.0))
     q = iota((pairs, DEPTH), 1)
     p = iota((pairs, DEPTH), 0)
-    r = jnp.where(q >= GROUP, q - GROUP, q)
-    r = jnp.where(r >= GROUP, r - GROUP, r)
-    hit = lax.shift_right_logical(r, 3) == p
-    to_high = jnp.where(hit & (q < 2 * GROUP), 1.0, 0.0).astype(BF16)
-    to_low = jnp.where(hit & (q >= 2 * GROUP) & (q < 3 * GROUP), 1.0, 0.0).astype(BF16)
-    wide = (dot(high, to_high) + dot(low, to_low)).astype(BF16)
-    wk_ref[...] = spread(wide)
-
-
-def spread(wide):
-    snaps, n = wide.shape
-    rows = 8 * snaps
-    e = (lax.shift_right_logical(iota((rows, snaps), 0), 3) == iota((rows, snaps), 1))
-    tall = dot(jnp.where(e, 1.0, 0.0).astype(BF16), wide)
-    same = (iota((rows, n), 0) & 7) == (iota((rows, n), 1) & 7)
-    return jnp.where(same, tall, 0.0).astype(BF16)
-
-
-def compute_kernel(fields, xb, xa, yb, ya, zb, za, wk_ref, sh_ref, sl_ref, g_ref, ypad):
+    r = jnp.where(q >= 2 * GROUP, q - 2 * GROUP, jnp.where(q >= GROUP, q - GROUP, q))
+    wanted = jnp.where(r < 72, 9 * lax.shift_right_logical(r, 3) + (r & 7), 9 * (r - 72) + 8)
+    wanted = jnp.where(q >= 3 * GROUP, pairs - 1, wanted)
+    use_low = ((q >= 2 * GROUP) & (q < 3 * GROUP)) | (q == 3 * GROUP + 2)
+    hit = (wanted == p) & (q < 3 * GROUP + 3)
+    to_high = jnp.where(hit & ~use_low, 1.0, 0.0).astype(BF16)
+    to_low = jnp.where(hit & use_low, 1.0, 0.0).astype(BF16)
+    wk_ref[...] = (dot(high, to_high) + dot(low, to_low)).astype(BF16)
+
+
+def compute_kernel(fields, xb, xa, yb, ya, zb, za, wk_ref, sh_ref, sl_ref, g_ref, ypad, grads):
     planes, rows = fields.shape[1], fields.shape[2]
     halves = rows // 8
     lane = iota((8, 128), 1)
@@ -118,43 +110,43 @@
         dn2 = jnp.where(lane >= 126, pltpu.roll(after, (124 - at) % 128, 1), pltpu.roll(tile, 126, 1))
         return 8.0 * (dn1 - up1) - (dn2 - up2)
 
+    lines = planes * rows
+    third = iota((16, 128), 0)
     for plane in range(planes):
-        slopes = []
         for comp in range(6):
             dx = 8.0 * (line(comp, plane + 1) - line(comp, plane - 1)) - (
                 line(comp, plane + 2) - line(comp, plane - 2)
             )
             y = lambda k: ypad[comp, plane, 8 + k : 8 + k + rows, :]
             dy = 8.0 * (y(1) - y(-1)) - (y(2) - y(-2))
-            dx = jnp.concatenate([dx[8 * h : 8 * h + 8] for h in range(halves)], 1)
-            dy = jnp.concatenate([dy[8 * h : 8 * h + 8] for h in range(halves)], 1)
-            dz = jnp.concatenate([depth_slope(comp, plane, h) for h in range(halves)], 1)
-            slopes += [dx, dy, dz]
-        products = [slopes[a] * slopes[9 + b] for a in range(9) for b in range(9)]
-        products.append(jnp.zeros_like(products[0]))
-        high, low = split(jnp.concatenate(products, 0))
-        rest = jnp.zeros((DEPTH - 3 * GROUP, high.shape[1]), BF16)
-        block = dot(wk_ref[...], jnp.concatenate([high, low, high, rest], 0))
-        high, low = split(block)
-        sh_ref[plane] = high
-        sl_ref[plane] = low
-        part = dot_nt(jnp.concatenate([high, low], 0), high)
-        total = part if total is None else total + part
-
-    n = total.shape[1]
-    same = (iota((n, n), 0) & 7) == (iota((n, n), 1) & 7)
-    main = jnp.where(same, total[:n] + total[n:], 0.0)
-    cross = jnp.where(same, total[n:], 0.0).astype(BF16)
-    snaps = n // 8
-    et = jnp.where(
-        lax.shift_right_logical(iota((snaps, n), 1), 3) == iota((snaps, n), 0), 1.0, 0.0
-    )
-    narrow = jnp.dot(et, main, precision=lax.Precision.HIGHEST, preferred_element_type=F32)
-    narrow = narrow + dot_nt(et.astype(BF16), cross)
-    tiled = jnp.where(
-        lax.shift_right_logical(iota((n, 128), 0), 3) == (iota((n, 128), 1) & 31), 1.0, 0.0
-    )
-    gram = jnp.dot(narrow, tiled, precision=lax.Precision.HIGHEST, preferred_element_type=F32)
+            dz = jnp.concatenate([depth_slope(comp, plane, h) for h in range(halves)], 0)
+            for dim, slope in enumerate((dx, dy, dz)):
+                at = (3 * comp + dim) * lines + plane * rows
+                grads[at : at + rows, :] = slope
+        for first in range(plane * rows, (plane + 1) * rows, 2):
+            columns = []
+            for at in (first, first + 1):
+                one = lambda entry: grads[entry * lines + at : entry * lines + at + 1, :]
+                forward = grads[pl.ds(at, 8, stride=lines), :]
+                adjoint = grads[pl.ds(9 * lines + at, 8, stride=lines), :]
+                products = [one(a) * adjoint for a in range(9)] + [forward * one(17)]
+                high, low = split(jnp.concatenate(products, 0))
+                final = jnp.broadcast_to(one(8) * one(17), third.shape)
+                final_high = final.astype(BF16).astype(F32)
+                final = jnp.where(third == 1, final - final_high, final_high)
+                final = jnp.where(third < 3, final, 0.0).astype(BF16)
+                columns.append(jnp.concatenate([high, low, high, final], 0))
+            block = dot(wk_ref[...], jnp.concatenate(columns, 1))
+            high, low = split(block)
+            sh_ref[:, 128 * first : 128 * first + 256] = high
+            sl_ref[:, 128 * first : 128 * first + 256] = low
+            both = jnp.concatenate([high, low], 0)
+            part = dot_nt(both, jnp.concatenate([both, both], 0))
+            total = part if total is None else total + part
+
+    snaps = total.shape[0] // 2
+    gram = total[:snaps] + total[snaps:]
+    gram = gram + pltpu.roll(gram, snaps, 1)
     packed = gram[0:8]
     for k in range(1, snaps // 8):
         packed = jnp.where(lane >= 32 * k, gram[8 * k : 8 * k + 8], packed)
@@ -182,9 +174,8 @@
     return jnp.where(lane < snaps, pltpu.roll(work, 128 - snaps, 1), 0.0)
 
 
-def basis_kernel(cells, r_ref, sh_ref, sl_ref, o_hbm, lk_ref, out_ref, sems):
-    planes, n = sh_ref.shape[:2]
-    snaps = n // 8
+def basis_kernel(cells, r_ref, sh_ref, sl_ref, o_hbm, out_ref, sems):
+    planes, snaps, rows, cols = out_ref.shape
     packed = r_ref[0]
     for i in range(1, r_ref.shape[0]):
         packed = packed + r_ref[i]
@@ -192,23 +183,20 @@
     gram = jnp.concatenate(
         [packed] + [pltpu.roll(packed, 128 - 32 * k, 1) for k in range(1, snaps // 8)], 0
     )
-    high, low = split(inverse_factor(gram, snaps))
-    to_wide = jnp.where(
-        lax.shift_right_logical(iota((128, n), 1), 3) == iota((128, n), 0), 1.0, 0.0
-    ).astype(BF16)
-    high = spread(dot(high, to_wide).astype(BF16))
-    low = spread(dot(low, to_wide).astype(BF16))
-    lk_ref[:, 0:n] = high
-    lk_ref[:, n : 2 * n] = high
-    lk_ref[:, 2 * n : 3 * n] = low
+    inverse = inverse_factor(gram, snaps)
+    high = inverse.astype(BF16).astype(F32)
+    low = inverse - high
+    factor = high + pltpu.roll(high, snaps, 1)
+    factor = factor + pltpu.roll(low, 2 * snaps, 1) + pltpu.roll(low, 3 * snaps, 1)
+    factor = factor.astype(BF16)
 
     copies = []
     for plane in range(planes):
-        high = sh_ref[plane]
-        out = dot(lk_ref[...], jnp.concatenate([high, sl_ref[plane], high], 0))
-        for half in range(out_ref.shape[2] // 8):
-            part = out[:, 128 * half : 128 * half + 128]
-            out_ref[plane, :, 8 * half : 8 * half + 8, :] = part.reshape(snaps, 8, 128)
+        part = slice(plane * rows * cols, (plane + 1) * rows * cols)
+        both = jnp.concatenate([sh_ref[:, part], sl_ref[:, part]], 0)
+        out = dot(factor, jnp.concatenate([both, both], 0))
+        for y in range(rows):
+            out_ref[plane, :, y, :] = out[:, cols * y : cols * y + cols]
         copy = pltpu.make_async_copy(out_ref.at[plane], o_hbm.at[:, plane], sems.at[plane])
         copy.start()
         copies.append(copy)
@@ -223,8 +211,7 @@
 def body(forward_velocity, adjoint_velocity, weights):
     _, planes, rows, cols = forward_velocity.shape
     snaps = weights.shape[0]
-    n = 8 * snaps
-    width = rows // 8 * cols
+    cells = planes * rows * cols
     zrows = -(-6 * planes * (rows // 8) * 4 // 128) * 8
     params = pltpu.CompilerParams(vmem_limit_bytes=48 * 2**20)
 
@@ -259,7 +246,7 @@
         weights_kernel,
         in_specs=[VMEM],
         out_specs=VMEM,
-        out_shape=shape(n, DEPTH, dtype=BF16),
+        out_shape=shape(snaps, DEPTH, dtype=BF16),
         compiler_params=params,
         interpret=INTERPRET,
     )(w)
@@ -271,11 +258,14 @@
         in_specs=[VMEM] * 8,
         out_specs=[VMEM] * 3,
         out_shape=[
-            shape(planes, n, width, dtype=BF16),
-            shape(planes, n, width, dtype=BF16),
+            shape(snaps, cells, dtype=BF16),
+            shape(snaps, cells, dtype=BF16),
             shape(span, 8, 128),
         ],
-        scratch_shapes=[pltpu.VMEM((6, planes, rows + 16, cols), F32)],
+        scratch_shapes=[
+            pltpu.VMEM((6, planes, rows + 16, cols), F32),
+            pltpu.VMEM((18 * planes * rows, cols), F32),
+        ],
         compiler_params=params,
         interpret=INTERPRET,
     )(fields, xb, xa, yb, ya, zb, za, wk)
@@ -284,14 +274,12 @@
     grams = jnp.broadcast_to(grams.sum(0)[None], (others, 8, 128))
     grams = lax.all_to_all(grams, ("stream", "depth"), 0, 0, tiled=True)
 
-    cells = planes * rows * cols * span * others
     return pl.pallas_call(
-        functools.partial(basis_kernel, cells),
+        functools.partial(basis_kernel, cells * span * others),
         in_specs=[VMEM] * 3,
         out_specs=HBM,
         out_shape=shape(snaps, planes, rows, cols),
         scratch_shapes=[
-            pltpu.VMEM((n, 3 * n), BF16),
             pltpu.VMEM((planes, snaps, rows, cols), F32),
             pltpu.SemaphoreType.DMA((planes,)),
         ],

time: 66.7 us -> 65.4 us (0.981)
  Pallas kernels: 9.29 us -> 7.5 us
    pallas_call x1, Pallas kernels: 4.44 us -> 2.79 us  [body(): pl.pallas_call(compute_kernel, in_specs=[VMEM] * 8, out_specs=[VMEM] * 3,...]
  transfers between devices with their start and end apart: 6 -> 6, of which waited for: 1 -> 1; matrix products, arithmetic and copies ran while one was open for 0% -> 0% of each run, Pallas kernels for 1% -> 0%
where the time goes in v3:
time: 65.4 us; the launch traced here: 65.1 us
  blocking collectives  34.2 us (52%)
  starting transfers between devices  22.1 us (34%)
  Pallas kernels  7.5 us (11%)
  waiting for transfers between devices  1.19 us (2%)
    ppermute x6, starting transfers between devices, move(): lax.ppermute(value, axis, [(i, (i + step) % size) for i in range(size)])  22.1 us
    all_to_all x1, blocking collectives, body(): grams = lax.all_to_all(grams, 'span', 0, 0, tiled=True)  17.6 us
    all_to_all x1, blocking collectives, body(): grams = lax.all_to_all(grams, ('stream', 'depth'), 0, 0, tiled=True)  16.6 us
    pallas_call x1, Pallas kernels, body(): pl.pallas_call(functools.partial(basis_kernel, cells * span * others), in...  3.31 us
    pallas_call x1, Pallas kernels, body(): pl.pallas_call(compute_kernel, in_specs=[VMEM] * 8, out_specs=[VMEM] * 3,...  2.79 us
  transfers between devices with their start and end apart: 6, of which 1 were waited for; matrix products, arithmetic and copies ran while one was open for 0% of the time, Pallas kernels for 0%

profile of v3, /device:TPU:1, one launch (start us, length us, event | category | flops | bytes accessed | tf_op | source)
XLA Modules:
  0.0 65.1 jit_solution(11426689765183509236)
XLA Ops:
  0.0 1.3 %shard_map.37 = (f32[6,8,16,128]{3,2,1,0:T(8,128)S(1)}, f32[32,81]{1,0:T(8,128)S(1)}, f32[6,2,16,128]{3,2,1,0:T(8,128)S(1)}, f32[6,2,16,128]{3,2,1,0:T(8,128)S(1...) custom-call(f32[3,8,16,128]{3,2,1,0:T(8,128)} %f_hbm.1, ...), custom_call_target="tpu_custom_call" | custom-call | tf_op jit(solution)/shard_map/pallas_call | solution.py:218
  1.3 4.8 %collective-permute-start = (f32[6,2,16,128]{3,2,1,0:T(8,128)S(1)}, f32[6,2,16,128]{3,2,1,0:T(8,128)S(1)}, u32[]{:S(2)}, u32[]{:S(2)}) collective-permute-start(f32[6,2,16,128]{3,2,1,0:T(8,128)S(1)} %get-tuple-element.18), channel_id=1, source_target_pairs={{0,64},{64,128},{128,192},{192,256},{256,320},{320,384},{384,448},... | collective-permute-start | bytes 294920 | tf_op jit(solution)/shard_map/ppermute | solution.py:238
  6.1 8.6 %collective-permute-start.1 = (f32[6,2,16,128]{3,2,1,0:T(8,128)S(1)}, f32[6,2,16,128]{3,2,1,0:T(8,128)S(1)}, u32[]{:S(2)}, u32[]{:S(2)}) collective-permute-start(f32[6,2,16,128]{3,2,1,0:T(8,128)S(1)} %get-tuple-element.19), channel_id=1, source_target_pairs={{0,448},{64,0},{128,64},{192,128},{256,192},{320,256},{384,320},{4... | collective-permute-start | bytes 294920 | tf_op jit(solution)/shard_map/ppermute | solution.py:238
  14.7 2.1 %collective-permute-start.2 = (f32[6,8,2,128]{3,2,1,0:T(2,128)S(1)}, f32[6,8,2,128]{3,2,1,0:T(2,128)S(1)}, u32[]{:S(2)}, u32[]{:S(2)}) collective-permute-start(f32[6,8,2,128]{3,2,1,0:T(2,128)S(1)} %get-tuple-element.20), channel_id=1, source_target_pairs={{0,4},{4,8},{8,12},{12,16},{16,20},{20,24},{24,28},{28,32},{32,36}... | collective-permute-start | bytes 147464 | tf_op jit(solution)/shard_map/ppermute | solution.py:238
  16.8 0.0 collective-permute-start.3
  16.9 0.0 collective-permute-done.xb
  16.9 3.1 %collective-permute-start.4 = (f32[24,128]{1,0:T(8,128)S(1)}, f32[24,128]{1,0:T(8,128)S(1)}, u32[]{:S(2)}, u32[]{:S(2)}) collective-permute-start(f32[24,128]{1,0:T(8,128)S(1)} %get-tuple-element.24), channel_id=1, source_target_pairs={{0,1},{1,2},{2,3},{3,0},{4,5},{5,6},{6,7},{7,4},{8,9},{9,10},{10,1... | collective-permute-start | bytes 36872 | tf_op jit(solution)/shard_map/ppermute | solution.py:238
  20.0 0.0 collective-permute-done.1.xa
  20.0 3.4 %collective-permute-start.5 = (f32[24,128]{1,0:T(8,128)S(1)}, f32[24,128]{1,0:T(8,128)S(1)}, u32[]{:S(2)}, u32[]{:S(2)}) collective-permute-start(f32[24,128]{1,0:T(8,128)S(1)} %get-tuple-element.24), channel_id=1, source_target_pairs={{0,3},{1,0},{2,1},{3,2},{4,7},{5,4},{6,5},{7,6},{8,11},{9,8},{10,9... | collective-permute-start | bytes 36872 | tf_op jit(solution)/shard_map/ppermute | solution.py:238
  23.4 0.1 shard_map.38.wk_ref
  23.5 0.0 collective-permute-done.2.yb
  23.5 0.0 collective-permute-done.3.ya
  23.5 0.0 collective-permute-done.4.zb
  23.5 1.2 %collective-permute-done.5.za = f32[24,128]{1,0:T(8,128)S(1)} collective-permute-done((f32[24,128]{1,0:T(8,128)S(1)}, f32[24,128]{1,0:T(8,128)S(1)}, u32[]{:S(2)}, u32[]{:S(2)}) %collective-permute-start.5) | collective-permute-done | bytes 12320 | tf_op jit(solution)/shard_map/ppermute | solution.py:238
  24.7 2.8 %shard_map.39 = (bf16[32,16384]{1,0:T(8,128)(2,1)S(1)}, bf16[32,16384]{1,0:T(8,128)(2,1)S(1)}, f32[16,8,128]{2,1,0:T(8,128)S(1)}) custom-call(f32[6,8,16,128]{3,2,1,0:T(8,128)S(1)} %get-tuple-element.17.fields, f32[6,2,16,128]{3,2,1,0:T(8,128)S(1)} %collective-permute-done.xb, f32[6,2,16,128]{3,2,1,0:T(8,128)S(1)} %collective-permute-done.1.xa, ...), custom_call_target="tpu_custom_call" | custom-call | tf_op jit(solution)/shard_map/pallas_call | solution.py:256
  27.5 17.6 %all_to_all.10 = f32[16,8,128]{2,1,0:T(8,128)S(1)} all-to-all(f32[16,8,128]{2,1,0:T(8,128)S(1)} %get-tuple-element.26), channel_id=1, replica_groups=mesh['stream'=8,'span'=16,'depth'=4] {'span'}, dimensions={0} | all-to-all | bytes 131072 | tf_op jit(solution)/shard_map/all_to_all | solution.py:273
  45.2 16.6 %all_to_all.11.r_ref = f32[32,8,128]{2,1,0:T(8,128)S(1)} all-to-all(f32[32,8,128]{2,1,0:T(8,128)S(1)} %broadcast_in_dim.2), channel_id=1, replica_groups=mesh['stream'=8,'span'=16,'depth'=4] {'stream','depth'}, dimensions={0} | all-to-all | bytes 262144 | tf_op jit(solution)/shard_map/all_to_all | solution.py:275
  61.8 3.3 %shard_map.40 = f32[32,8,16,128]{3,2,1,0:T(8,128)} custom-call(f32[32,8,128]{2,1,0:T(8,128)S(1)} %all_to_all.11.r_ref, bf16[32,16384]{1,0:T(8,128)(2,1)S(1)} %get-tuple-element.27.sh_ref, bf16[32,16384]{1,0:T(8,128)(2,1)S(1)} %get-tuple-element.28.sl_ref), custom_call_target="tpu_custom_call" | custom-call | tf_op jit(solution)/shard_map/pallas_call | solution.py:277
  (2 shorter events, 0.0 us)
Async XLA Ops:
  1.3 15.6 %collective-permute-start = (f32[6,2,16,128]{3,2,1,0:T(8,128)S(1)}, f32[6,2,16,128]{3,2,1,0:T(8,128)S(1)}, u32[]{:S(2)}, u32[]{:S(2)}) collective-permute-start(f32[6,2,16,128]{3,2,1,0:T(8,128)S(1)} %get-tuple-element.18), channel_id=1, source_target_pairs={{0,64},{64,128},{128,192},{192,256},{256,320},{320,384},{384,448},... | collective-permute-start | bytes 294920 | tf_op jit(solution)/shard_map/ppermute | solution.py:238
  6.1 13.9 %collective-permute-start.1 = (f32[6,2,16,128]{3,2,1,0:T(8,128)S(1)}, f32[6,2,16,128]{3,2,1,0:T(8,128)S(1)}, u32[]{:S(2)}, u32[]{:S(2)}) collective-permute-start(f32[6,2,16,128]{3,2,1,0:T(8,128)S(1)} %get-tuple-element.19), channel_id=1, source_target_pairs={{0,448},{64,0},{128,64},{192,128},{256,192},{320,256},{384,320},{4... | collective-permute-start | bytes 294920 | tf_op jit(solution)/shard_map/ppermute | solution.py:238
  14.7 8.8 %collective-permute-start.2 = (f32[6,8,2,128]{3,2,1,0:T(2,128)S(1)}, f32[6,8,2,128]{3,2,1,0:T(2,128)S(1)}, u32[]{:S(2)}, u32[]{:S(2)}) collective-permute-start(f32[6,8,2,128]{3,2,1,0:T(2,128)S(1)} %get-tuple-element.20), channel_id=1, source_target_pairs={{0,4},{4,8},{8,12},{12,16},{16,20},{20,24},{24,28},{28,32},{32,36}... | collective-permute-start | bytes 147464 | tf_op jit(solution)/shard_map/ppermute | solution.py:238
  16.8 6.7 %collective-permute-start.3 = (f32[6,8,2,128]{3,2,1,0:T(2,128)S(1)}, f32[6,8,2,128]{3,2,1,0:T(2,128)S(1)}, u32[]{:S(2)}, u32[]{:S(2)}) collective-permute-start(f32[6,8,2,128]{3,2,1,0:T(2,128)S(1)} %get-tuple-element.21), channel_id=1, source_target_pairs={{0,60},{4,0},{8,4},{12,8},{16,12},{20,16},{24,20},{28,24},{32,28},... | collective-permute-start | bytes 147464 | tf_op jit(solution)/shard_map/ppermute | solution.py:238
  16.9 6.7 %collective-permute-start.4 = (f32[24,128]{1,0:T(8,128)S(1)}, f32[24,128]{1,0:T(8,128)S(1)}, u32[]{:S(2)}, u32[]{:S(2)}) collective-permute-start(f32[24,128]{1,0:T(8,128)S(1)} %get-tuple-element.24), channel_id=1, source_target_pairs={{0,1},{1,2},{2,3},{3,0},{4,5},{5,6},{6,7},{7,4},{8,9},{9,10},{10,1... | collective-permute-start | bytes 36872 | tf_op jit(solution)/shard_map/ppermute | solution.py:238
  20.0 4.7 %collective-permute-start.5 = (f32[24,128]{1,0:T(8,128)S(1)}, f32[24,128]{1,0:T(8,128)S(1)}, u32[]{:S(2)}, u32[]{:S(2)}) collective-permute-start(f32[24,128]{1,0:T(8,128)S(1)} %get-tuple-element.24), channel_id=1, source_target_pairs={{0,3},{1,0},{2,1},{3,2},{4,7},{5,4},{6,5},{7,6},{8,11},{9,8},{10,9... | collective-permute-start | bytes 36872 | tf_op jit(solution)/shard_map/ppermute | solution.py:238

commit v4 on v3

--- a/solution.py
+++ b/solution.py
@@ -190,13 +190,14 @@
     factor = factor + pltpu.roll(low, 2 * snaps, 1) + pltpu.roll(low, 3 * snaps, 1)
     factor = factor.astype(BF16)
 
+    flat = out_ref.reshape(planes * snaps * rows, cols)
     copies = []
     for plane in range(planes):
         part = slice(plane * rows * cols, (plane + 1) * rows * cols)
         both = jnp.concatenate([sh_ref[:, part], sl_ref[:, part]], 0)
         out = dot(factor, jnp.concatenate([both, both], 0))
         for y in range(rows):
-            out_ref[plane, :, y, :] = out[:, cols * y : cols * y + cols]
+            flat[pl.ds(plane * snaps * rows + y, snaps, stride=rows), :] = out[:, cols * y : cols * y + cols]
         copy = pltpu.make_async_copy(out_ref.at[plane], o_hbm.at[:, plane], sems.at[plane])
         copy.start()
         copies.append(copy)

time: 65.4 us -> 64.6 us (0.988)
  Pallas kernels: 7.5 us -> 6.75 us
    pallas_call x1, Pallas kernels: 3.31 us -> 2.56 us  [body(): pl.pallas_call(functools.partial(basis_kernel, cells * span * others), in...]
where the time goes in v4:
time: 64.6 us; the launch traced here: 64.3 us
  blocking collectives  34.2 us (53%)
  starting transfers between devices  22.1 us (34%)
  Pallas kernels  6.75 us (10%)
  waiting for transfers between devices  1.19 us (2%)
    ppermute x6, starting transfers between devices, move(): lax.ppermute(value, axis, [(i, (i + step) % size) for i in range(size)])  22.1 us
    all_to_all x1, blocking collectives, body(): grams = lax.all_to_all(grams, 'span', 0, 0, tiled=True)  17.6 us
    all_to_all x1, blocking collectives, body(): grams = lax.all_to_all(grams, ('stream', 'depth'), 0, 0, tiled=True)  16.6 us
    pallas_call x1, Pallas kernels, body(): pl.pallas_call(compute_kernel, in_specs=[VMEM] * 8, out_specs=[VMEM] * 3,...  2.79 us
    pallas_call x1, Pallas kernels, body(): pl.pallas_call(functools.partial(basis_kernel, cells * span * others), in...  2.56 us
  transfers between devices with their start and end apart: 6, of which 1 were waited for; matrix products, arithmetic and copies ran while one was open for 0% of the time, Pallas kernels for 0%

profile of v4, /device:TPU:1, one launch (start us, length us, event | category | flops | bytes accessed | tf_op | source)
XLA Modules:
  0.0 64.3 jit_solution(5941799981578715554)
XLA Ops:
  0.0 1.3 %shard_map.37 = (f32[6,8,16,128]{3,2,1,0:T(8,128)S(1)}, f32[32,81]{1,0:T(8,128)S(1)}, f32[6,2,16,128]{3,2,1,0:T(8,128)S(1)}, f32[6,2,16,128]{3,2,1,0:T(8,128)S(1...) custom-call(f32[3,8,16,128]{3,2,1,0:T(8,128)} %f_hbm.1, ...), custom_call_target="tpu_custom_call" | custom-call | tf_op jit(solution)/shard_map/pallas_call | solution.py:219
  1.3 4.8 %collective-permute-start = (f32[6,2,16,128]{3,2,1,0:T(8,128)S(1)}, f32[6,2,16,128]{3,2,1,0:T(8,128)S(1)}, u32[]{:S(2)}, u32[]{:S(2)}) collective-permute-start(f32[6,2,16,128]{3,2,1,0:T(8,128)S(1)} %get-tuple-element.18), channel_id=1, source_target_pairs={{0,64},{64,128},{128,192},{192,256},{256,320},{320,384},{384,448},... | collective-permute-start | bytes 294920 | tf_op jit(solution)/shard_map/ppermute | solution.py:239
  6.1 8.6 %collective-permute-start.1 = (f32[6,2,16,128]{3,2,1,0:T(8,128)S(1)}, f32[6,2,16,128]{3,2,1,0:T(8,128)S(1)}, u32[]{:S(2)}, u32[]{:S(2)}) collective-permute-start(f32[6,2,16,128]{3,2,1,0:T(8,128)S(1)} %get-tuple-element.19), channel_id=1, source_target_pairs={{0,448},{64,0},{128,64},{192,128},{256,192},{320,256},{384,320},{4... | collective-permute-start | bytes 294920 | tf_op jit(solution)/shard_map/ppermute | solution.py:239
  14.7 2.1 %collective-permute-start.2 = (f32[6,8,2,128]{3,2,1,0:T(2,128)S(1)}, f32[6,8,2,128]{3,2,1,0:T(2,128)S(1)}, u32[]{:S(2)}, u32[]{:S(2)}) collective-permute-start(f32[6,8,2,128]{3,2,1,0:T(2,128)S(1)} %get-tuple-element.20), channel_id=1, source_target_pairs={{0,4},{4,8},{8,12},{12,16},{16,20},{20,24},{24,28},{28,32},{32,36}... | collective-permute-start | bytes 147464 | tf_op jit(solution)/shard_map/ppermute | solution.py:239
  16.8 0.0 collective-permute-start.3
  16.9 0.0 collective-permute-done.xb
  16.9 3.1 %collective-permute-start.4 = (f32[24,128]{1,0:T(8,128)S(1)}, f32[24,128]{1,0:T(8,128)S(1)}, u32[]{:S(2)}, u32[]{:S(2)}) collective-permute-start(f32[24,128]{1,0:T(8,128)S(1)} %get-tuple-element.24), channel_id=1, source_target_pairs={{0,1},{1,2},{2,3},{3,0},{4,5},{5,6},{6,7},{7,4},{8,9},{9,10},{10,1... | collective-permute-start | bytes 36872 | tf_op jit(solution)/shard_map/ppermute | solution.py:239
  20.0 0.0 collective-permute-done.1.xa
  20.0 3.4 %collective-permute-start.5 = (f32[24,128]{1,0:T(8,128)S(1)}, f32[24,128]{1,0:T(8,128)S(1)}, u32[]{:S(2)}, u32[]{:S(2)}) collective-permute-start(f32[24,128]{1,0:T(8,128)S(1)} %get-tuple-element.24), channel_id=1, source_target_pairs={{0,3},{1,0},{2,1},{3,2},{4,7},{5,4},{6,5},{7,6},{8,11},{9,8},{10,9... | collective-permute-start | bytes 36872 | tf_op jit(solution)/shard_map/ppermute | solution.py:239
  23.4 0.1 shard_map.38.wk_ref
  23.5 0.0 collective-permute-done.2.yb
  23.5 0.0 collective-permute-done.3.ya
  23.5 0.0 collective-permute-done.4.zb
  23.5 1.2 %collective-permute-done.5.za = f32[24,128]{1,0:T(8,128)S(1)} collective-permute-done((f32[24,128]{1,0:T(8,128)S(1)}, f32[24,128]{1,0:T(8,128)S(1)}, u32[]{:S(2)}, u32[]{:S(2)}) %collective-permute-start.5) | collective-permute-done | bytes 12320 | tf_op jit(solution)/shard_map/ppermute | solution.py:239
  24.7 2.8 %shard_map.39 = (bf16[32,16384]{1,0:T(8,128)(2,1)S(1)}, bf16[32,16384]{1,0:T(8,128)(2,1)S(1)}, f32[16,8,128]{2,1,0:T(8,128)S(1)}) custom-call(f32[6,8,16,128]{3,2,1,0:T(8,128)S(1)} %get-tuple-element.17.fields, f32[6,2,16,128]{3,2,1,0:T(8,128)S(1)} %collective-permute-done.xb, f32[6,2,16,128]{3,2,1,0:T(8,128)S(1)} %collective-permute-done.1.xa, ...), custom_call_target="tpu_custom_call" | custom-call | tf_op jit(solution)/shard_map/pallas_call | solution.py:257
  27.5 17.6 %all_to_all.10 = f32[16,8,128]{2,1,0:T(8,128)S(1)} all-to-all(f32[16,8,128]{2,1,0:T(8,128)S(1)} %get-tuple-element.26), channel_id=1, replica_groups=mesh['stream'=8,'span'=16,'depth'=4] {'span'}, dimensions={0} | all-to-all | bytes 131072 | tf_op jit(solution)/shard_map/all_to_all | solution.py:274
  45.2 16.6 %all_to_all.11.r_ref = f32[32,8,128]{2,1,0:T(8,128)S(1)} all-to-all(f32[32,8,128]{2,1,0:T(8,128)S(1)} %broadcast_in_dim.2), channel_id=1, replica_groups=mesh['stream'=8,'span'=16,'depth'=4] {'stream','depth'}, dimensions={0} | all-to-all | bytes 262144 | tf_op jit(solution)/shard_map/all_to_all | solution.py:276
  61.8 2.6 %shard_map.40 = f32[32,8,16,128]{3,2,1,0:T(8,128)} custom-call(f32[32,8,128]{2,1,0:T(8,128)S(1)} %all_to_all.11.r_ref, bf16[32,16384]{1,0:T(8,128)(2,1)S(1)} %get-tuple-element.27.sh_ref, bf16[32,16384]{1,0:T(8,128)(2,1)S(1)} %get-tuple-element.28.sl_ref), custom_call_target="tpu_custom_call" | custom-call | tf_op jit(solution)/shard_map/pallas_call | solution.py:278
  (2 shorter events, 0.0 us)
Async XLA Ops:
  1.3 15.6 %collective-permute-start = (f32[6,2,16,128]{3,2,1,0:T(8,128)S(1)}, f32[6,2,16,128]{3,2,1,0:T(8,128)S(1)}, u32[]{:S(2)}, u32[]{:S(2)}) collective-permute-start(f32[6,2,16,128]{3,2,1,0:T(8,128)S(1)} %get-tuple-element.18), channel_id=1, source_target_pairs={{0,64},{64,128},{128,192},{192,256},{256,320},{320,384},{384,448},... | collective-permute-start | bytes 294920 | tf_op jit(solution)/shard_map/ppermute | solution.py:239
  6.1 13.9 %collective-permute-start.1 = (f32[6,2,16,128]{3,2,1,0:T(8,128)S(1)}, f32[6,2,16,128]{3,2,1,0:T(8,128)S(1)}, u32[]{:S(2)}, u32[]{:S(2)}) collective-permute-start(f32[6,2,16,128]{3,2,1,0:T(8,128)S(1)} %get-tuple-element.19), channel_id=1, source_target_pairs={{0,448},{64,0},{128,64},{192,128},{256,192},{320,256},{384,320},{4... | collective-permute-start | bytes 294920 | tf_op jit(solution)/shard_map/ppermute | solution.py:239
  14.7 8.8 %collective-permute-start.2 = (f32[6,8,2,128]{3,2,1,0:T(2,128)S(1)}, f32[6,8,2,128]{3,2,1,0:T(2,128)S(1)}, u32[]{:S(2)}, u32[]{:S(2)}) collective-permute-start(f32[6,8,2,128]{3,2,1,0:T(2,128)S(1)} %get-tuple-element.20), channel_id=1, source_target_pairs={{0,4},{4,8},{8,12},{12,16},{16,20},{20,24},{24,28},{28,32},{32,36}... | collective-permute-start | bytes 147464 | tf_op jit(solution)/shard_map/ppermute | solution.py:239
  16.8 6.7 %collective-permute-start.3 = (f32[6,8,2,128]{3,2,1,0:T(2,128)S(1)}, f32[6,8,2,128]{3,2,1,0:T(2,128)S(1)}, u32[]{:S(2)}, u32[]{:S(2)}) collective-permute-start(f32[6,8,2,128]{3,2,1,0:T(2,128)S(1)} %get-tuple-element.21), channel_id=1, source_target_pairs={{0,60},{4,0},{8,4},{12,8},{16,12},{20,16},{24,20},{28,24},{32,28},... | collective-permute-start | bytes 147464 | tf_op jit(solution)/shard_map/ppermute | solution.py:239
  16.9 6.7 %collective-permute-start.4 = (f32[24,128]{1,0:T(8,128)S(1)}, f32[24,128]{1,0:T(8,128)S(1)}, u32[]{:S(2)}, u32[]{:S(2)}) collective-permute-start(f32[24,128]{1,0:T(8,128)S(1)} %get-tuple-element.24), channel_id=1, source_target_pairs={{0,1},{1,2},{2,3},{3,0},{4,5},{5,6},{6,7},{7,4},{8,9},{9,10},{10,1... | collective-permute-start | bytes 36872 | tf_op jit(solution)/shard_map/ppermute | solution.py:239
  20.0 4.7 %collective-permute-start.5 = (f32[24,128]{1,0:T(8,128)S(1)}, f32[24,128]{1,0:T(8,128)S(1)}, u32[]{:S(2)}, u32[]{:S(2)}) collective-permute-start(f32[24,128]{1,0:T(8,128)S(1)} %get-tuple-element.24), channel_id=1, source_target_pairs={{0,3},{1,0},{2,1},{3,2},{4,7},{5,4},{6,5},{7,6},{8,11},{9,8},{10,9... | collective-permute-start | bytes 36872 | tf_op jit(solution)/shard_map/ppermute | solution.py:239

commit v5 on v4

--- a/solution.py
+++ b/solution.py
@@ -147,10 +147,16 @@
     snaps = total.shape[0] // 2
     gram = total[:snaps] + total[snaps:]
     gram = gram + pltpu.roll(gram, snaps, 1)
-    packed = gram[0:8]
-    for k in range(1, snaps // 8):
-        packed = jnp.where(lane >= 32 * k, gram[8 * k : 8 * k + 8], packed)
-    g_ref[...] = jnp.broadcast_to(packed[None], g_ref.shape)
+    row, wide = iota((16, 128), 0), iota((16, 128), 1)
+    half = jnp.where(((wide - row) & 31) < 16, gram[0:16], gram[16:32])
+    middle = jnp.sum(jnp.where((wide & 31) == row + 16, gram[0:16], 0.0), axis=0, keepdims=True)
+    parts = [half[0:8], pltpu.roll(half[0:8], 4, 0), half[8:16], pltpu.roll(half[8:16], 4, 0)]
+    packed = parts[0]
+    for k in range(1, 4):
+        packed = jnp.where(lane >= 32 * k, parts[k], packed)
+    for j in range(5):
+        line = packed[j : j + 1] if j < 4 else middle
+        g_ref[:, :, 128 * j : 128 * j + 128] = jnp.broadcast_to(line[None], (g_ref.shape[0], 1, 128))
 
 
 def inverse_factor(gram, snaps):
@@ -180,9 +186,20 @@
     for i in range(1, r_ref.shape[0]):
         packed = packed + r_ref[i]
     packed = packed * (1.0 / cells)
-    gram = jnp.concatenate(
-        [packed] + [pltpu.roll(packed, 128 - 32 * k, 1) for k in range(1, snaps // 8)], 0
-    )
+    row8 = iota((8, 128), 0)
+    quad = jnp.zeros((8, 128), F32)
+    for j in range(4):
+        quad = jnp.where((row8 & 3) == j, packed[:, 128 * j : 128 * j + 128], quad)
+    turned = [quad] + [pltpu.roll(quad, 128 - 32 * k, 1) for k in range(1, 4)]
+    half = [jnp.where(row8 < 4, turned[2 * k], turned[2 * k + 1]) for k in range(2)]
+    half = jnp.concatenate(half + half, 0)
+    row, wide = iota((snaps, 128), 0), iota((snaps, 128), 1)
+    middle = (row < 16) & (wide == row + 16)
+    half = jnp.where(middle, packed[:, 512:640], half)
+    known = (wide < snaps) & (middle | (((wide - row) & 31) < 16))
+    half = jnp.where(known, half, 0.0)
+    mirror = jnp.concatenate([half, jnp.zeros((128 - snaps, 128), F32)], 0).T[0:snaps]
+    gram = jnp.where(known, half, mirror)
     inverse = inverse_factor(gram, snaps)
     high = inverse.astype(BF16).astype(F32)
     low = inverse - high
@@ -261,7 +278,7 @@
         out_shape=[
             shape(snaps, cells, dtype=BF16),
             shape(snaps, cells, dtype=BF16),
-            shape(span, 8, 128),
+            shape(span, 1, 640),
         ],
         scratch_shapes=[
             pltpu.VMEM((6, planes, rows + 16, cols), F32),
@@ -272,7 +289,7 @@
     )(fields, xb, xa, yb, ya, zb, za, wk)
 
     grams = lax.all_to_all(grams, "span", 0, 0, tiled=True)
-    grams = jnp.broadcast_to(grams.sum(0)[None], (others, 8, 128))
+    grams = jnp.broadcast_to(grams.sum(0)[None], (others, 1, 640))
     grams = lax.all_to_all(grams, ("stream", "depth"), 0, 0, tiled=True)
 
     return pl.pallas_call(

time: 64.6 us -> 63.6 us (0.985)
  blocking collectives: 34.2 us -> 33 us
    all_to_all x1, blocking collectives: 16.6 us -> 15.7 us  [body(): grams = lax.all_to_all(grams, ('stream', 'depth'), 0, 0, tiled=True)]
where the time goes in v5:
time: 63.6 us; the launch traced here: 63.3 us
  blocking collectives  33 us (52%)
  starting transfers between devices  22.1 us (35%)
  Pallas kernels  6.94 us (11%)
  waiting for transfers between devices  1.19 us (2%)
    ppermute x6, starting transfers between devices, move(): lax.ppermute(value, axis, [(i, (i + step) % size) for i in range(size)])  22.1 us
    all_to_all x1, blocking collectives, body(): grams = lax.all_to_all(grams, 'span', 0, 0, tiled=True)  17.2 us
    all_to_all x1, blocking collectives, body(): grams = lax.all_to_all(grams, ('stream', 'depth'), 0, 0, tiled=True)  15.7 us
    pallas_call x1, Pallas kernels, body(): pl.pallas_call(compute_kernel, in_specs=[VMEM] * 8, out_specs=[VMEM] * 3,...  2.85 us
    pallas_call x1, Pallas kernels, body(): pl.pallas_call(functools.partial(basis_kernel, cells * span * others), in...  2.69 us
  transfers between devices with their start and end apart: 6, of which 1 were waited for; matrix products, arithmetic and copies ran while one was open for 0% of the time, Pallas kernels for 0%

profile of v5, /device:TPU:1, one launch (start us, length us, event | category | flops | bytes accessed | tf_op | source)
XLA Modules:
  0.0 63.3 jit_solution(6181823514135521594)
XLA Ops:
  0.0 1.3 %shard_map.37 = (f32[6,8,16,128]{3,2,1,0:T(8,128)S(1)}, f32[32,81]{1,0:T(8,128)S(1)}, f32[6,2,16,128]{3,2,1,0:T(8,128)S(1)}, f32[6,2,16,128]{3,2,1,0:T(8,128)S(1...) custom-call(f32[3,8,16,128]{3,2,1,0:T(8,128)} %f_hbm.1, ...), custom_call_target="tpu_custom_call" | custom-call | tf_op jit(solution)/shard_map/pallas_call | solution.py:236
  1.3 4.8 %collective-permute-start = (f32[6,2,16,128]{3,2,1,0:T(8,128)S(1)}, f32[6,2,16,128]{3,2,1,0:T(8,128)S(1)}, u32[]{:S(2)}, u32[]{:S(2)}) collective-permute-start(f32[6,2,16,128]{3,2,1,0:T(8,128)S(1)} %get-tuple-element.18), channel_id=1, source_target_pairs={{0,64},{64,128},{128,192},{192,256},{256,320},{320,384},{384,448},... | collective-permute-start | bytes 294920 | tf_op jit(solution)/shard_map/ppermute | solution.py:256
  6.1 8.6 %collective-permute-start.1 = (f32[6,2,16,128]{3,2,1,0:T(8,128)S(1)}, f32[6,2,16,128]{3,2,1,0:T(8,128)S(1)}, u32[]{:S(2)}, u32[]{:S(2)}) collective-permute-start(f32[6,2,16,128]{3,2,1,0:T(8,128)S(1)} %get-tuple-element.19), channel_id=1, source_target_pairs={{0,448},{64,0},{128,64},{192,128},{256,192},{320,256},{384,320},{4... | collective-permute-start | bytes 294920 | tf_op jit(solution)/shard_map/ppermute | solution.py:256
  14.7 2.1 %collective-permute-start.2 = (f32[6,8,2,128]{3,2,1,0:T(2,128)S(1)}, f32[6,8,2,128]{3,2,1,0:T(2,128)S(1)}, u32[]{:S(2)}, u32[]{:S(2)}) collective-permute-start(f32[6,8,2,128]{3,2,1,0:T(2,128)S(1)} %get-tuple-element.20), channel_id=1, source_target_pairs={{0,4},{4,8},{8,12},{12,16},{16,20},{20,24},{24,28},{28,32},{32,36}... | collective-permute-start | bytes 147464 | tf_op jit(solution)/shard_map/ppermute | solution.py:256
  16.8 0.0 collective-permute-start.3
  16.9 0.0 collective-permute-done.xb
  16.9 3.1 %collective-permute-start.4 = (f32[24,128]{1,0:T(8,128)S(1)}, f32[24,128]{1,0:T(8,128)S(1)}, u32[]{:S(2)}, u32[]{:S(2)}) collective-permute-start(f32[24,128]{1,0:T(8,128)S(1)} %get-tuple-element.24), channel_id=1, source_target_pairs={{0,1},{1,2},{2,3},{3,0},{4,5},{5,6},{6,7},{7,4},{8,9},{9,10},{10,1... | collective-permute-start | bytes 36872 | tf_op jit(solution)/shard_map/ppermute | solution.py:256
  20.0 0.0 collective-permute-done.1.xa
  20.0 3.4 %collective-permute-start.5 = (f32[24,128]{1,0:T(8,128)S(1)}, f32[24,128]{1,0:T(8,128)S(1)}, u32[]{:S(2)}, u32[]{:S(2)}) collective-permute-start(f32[24,128]{1,0:T(8,128)S(1)} %get-tuple-element.24), channel_id=1, source_target_pairs={{0,3},{1,0},{2,1},{3,2},{4,7},{5,4},{6,5},{7,6},{8,11},{9,8},{10,9... | collective-permute-start | bytes 36872 | tf_op jit(solution)/shard_map/ppermute | solution.py:256
  23.4 0.1 shard_map.38.wk_ref
  23.5 0.0 collective-permute-done.2.yb
  23.5 0.0 collective-permute-done.3.ya
  23.5 0.0 collective-permute-done.4.zb
  23.5 1.2 %collective-permute-done.5.za = f32[24,128]{1,0:T(8,128)S(1)} collective-permute-done((f32[24,128]{1,0:T(8,128)S(1)}, f32[24,128]{1,0:T(8,128)S(1)}, u32[]{:S(2)}, u32[]{:S(2)}) %collective-permute-start.5) | collective-permute-done | bytes 12320 | tf_op jit(solution)/shard_map/ppermute | solution.py:256
  24.7 2.8 %shard_map.39 = (bf16[32,16384]{1,0:T(8,128)(2,1)S(1)}, bf16[32,16384]{1,0:T(8,128)(2,1)S(1)}, f32[16,1,640]{2,1,0:T(1,128)S(1)}) custom-call(f32[6,8,16,128]{3,2,1,0:T(8,128)S(1)} %get-tuple-element.17.fields, f32[6,2,16,128]{3,2,1,0:T(8,128)S(1)} %collective-permute-done.xb, f32[6,2,16,128]{3,2,1,0:T(8,128)S(1)} %collective-permute-done.1.xa, ...), custom_call_target="tpu_custom_call" | custom-call | tf_op jit(solution)/shard_map/pallas_call | solution.py:274
  27.6 17.2 %all_to_all.10 = f32[16,1,640]{2,1,0:T(1,128)S(1)} all-to-all(f32[16,1,640]{2,1,0:T(1,128)S(1)} %get-tuple-element.26), channel_id=1, replica_groups=mesh['stream'=8,'span'=16,'depth'=4] {'span'}, dimensions={0} | all-to-all | bytes 81920 | tf_op jit(solution)/shard_map/all_to_all | solution.py:291
  44.9 15.7 %all_to_all.11.r_ref = f32[32,1,640]{2,1,0:T(1,128)S(1)} all-to-all(f32[32,1,640]{2,1,0:T(1,128)S(1)} %broadcast_in_dim.2), channel_id=1, replica_groups=mesh['stream'=8,'span'=16,'depth'=4] {'stream','depth'}, dimensions={0} | all-to-all | bytes 163840 | tf_op jit(solution)/shard_map/all_to_all | solution.py:293
  60.6 2.7 %shard_map.40 = f32[32,8,16,128]{3,2,1,0:T(8,128)} custom-call(f32[32,1,640]{2,1,0:T(1,128)S(1)} %all_to_all.11.r_ref, bf16[32,16384]{1,0:T(8,128)(2,1)S(1)} %get-tuple-element.27.sh_ref, bf16[32,16384]{1,0:T(8,128)(2,1)S(1)} %get-tuple-element.28.sl_ref), custom_call_target="tpu_custom_call" | custom-call | tf_op jit(solution)/shard_map/pallas_call | solution.py:295
  (2 shorter events, 0.1 us)
Async XLA Ops:
  1.3 15.6 %collective-permute-start = (f32[6,2,16,128]{3,2,1,0:T(8,128)S(1)}, f32[6,2,16,128]{3,2,1,0:T(8,128)S(1)}, u32[]{:S(2)}, u32[]{:S(2)}) collective-permute-start(f32[6,2,16,128]{3,2,1,0:T(8,128)S(1)} %get-tuple-element.18), channel_id=1, source_target_pairs={{0,64},{64,128},{128,192},{192,256},{256,320},{320,384},{384,448},... | collective-permute-start | bytes 294920 | tf_op jit(solution)/shard_map/ppermute | solution.py:256
  6.1 13.9 %collective-permute-start.1 = (f32[6,2,16,128]{3,2,1,0:T(8,128)S(1)}, f32[6,2,16,128]{3,2,1,0:T(8,128)S(1)}, u32[]{:S(2)}, u32[]{:S(2)}) collective-permute-start(f32[6,2,16,128]{3,2,1,0:T(8,128)S(1)} %get-tuple-element.19), channel_id=1, source_target_pairs={{0,448},{64,0},{128,64},{192,128},{256,192},{320,256},{384,320},{4... | collective-permute-start | bytes 294920 | tf_op jit(solution)/shard_map/ppermute | solution.py:256
  14.7 8.8 %collective-permute-start.2 = (f32[6,8,2,128]{3,2,1,0:T(2,128)S(1)}, f32[6,8,2,128]{3,2,1,0:T(2,128)S(1)}, u32[]{:S(2)}, u32[]{:S(2)}) collective-permute-start(f32[6,8,2,128]{3,2,1,0:T(2,128)S(1)} %get-tuple-element.20), channel_id=1, source_target_pairs={{0,4},{4,8},{8,12},{12,16},{16,20},{20,24},{24,28},{28,32},{32,36}... | collective-permute-start | bytes 147464 | tf_op jit(solution)/shard_map/ppermute | solution.py:256
  16.8 6.7 %collective-permute-start.3 = (f32[6,8,2,128]{3,2,1,0:T(2,128)S(1)}, f32[6,8,2,128]{3,2,1,0:T(2,128)S(1)}, u32[]{:S(2)}, u32[]{:S(2)}) collective-permute-start(f32[6,8,2,128]{3,2,1,0:T(2,128)S(1)} %get-tuple-element.21), channel_id=1, source_target_pairs={{0,60},{4,0},{8,4},{12,8},{16,12},{20,16},{24,20},{28,24},{32,28},... | collective-permute-start | bytes 147464 | tf_op jit(solution)/shard_map/ppermute | solution.py:256
  16.9 6.7 %collective-permute-start.4 = (f32[24,128]{1,0:T(8,128)S(1)}, f32[24,128]{1,0:T(8,128)S(1)}, u32[]{:S(2)}, u32[]{:S(2)}) collective-permute-start(f32[24,128]{1,0:T(8,128)S(1)} %get-tuple-element.24), channel_id=1, source_target_pairs={{0,1},{1,2},{2,3},{3,0},{4,5},{5,6},{6,7},{7,4},{8,9},{9,10},{10,1... | collective-permute-start | bytes 36872 | tf_op jit(solution)/shard_map/ppermute | solution.py:256
  20.0 4.7 %collective-permute-start.5 = (f32[24,128]{1,0:T(8,128)S(1)}, f32[24,128]{1,0:T(8,128)S(1)}, u32[]{:S(2)}, u32[]{:S(2)}) collective-permute-start(f32[24,128]{1,0:T(8,128)S(1)} %get-tuple-element.24), channel_id=1, source_target_pairs={{0,3},{1,0},{2,1},{3,2},{4,7},{5,4},{6,5},{7,6},{8,11},{9,8},{10,9... | collective-permute-start | bytes 36872 | tf_op jit(solution)/shard_map/ppermute | solution.py:256

commit v6 on v5

--- a/solution.py
+++ b/solution.py
@@ -258,7 +258,7 @@
     xb, xa = move(xl, "stream", 1), move(xf, "stream", -1)
     yb, ya = move(yl, "span", 1), move(yf, "span", -1)
     zb = move(lax.optimization_barrier((zs, xb))[0], "depth", 1)
-    za = move(lax.optimization_barrier((zs, xa))[0], "depth", -1)
+    za = move(lax.optimization_barrier((zs, xb))[0], "depth", -1)
 
     wk = pl.pallas_call(
         weights_kernel,

time: 63.6 us -> 63.7 us (level)
  waiting for transfers between devices: 1.19 us -> 3.55 us
  blocking collectives: 33 us -> 30.9 us
    all_to_all x1, blocking collectives: 15.7 us -> 13.3 us  [body(): grams = lax.all_to_all(grams, ('stream', 'depth'), 0, 0, tiled=True)]
    ppermute x6, waiting for transfers between devices: 1.19 us -> 3.55 us  [move(): lax.ppermute(value, axis, [(i, (i + step) % size) for i in range(size)])]
where the time goes in v6:
time: 63.7 us; the launch traced here: 63.4 us
  blocking collectives  30.9 us (49%)
  starting transfers between devices  21.9 us (34%)
  Pallas kernels  6.94 us (11%)
  waiting for transfers between devices  3.55 us (6%)
    ppermute x6, starting transfers between devices, move(): lax.ppermute(value, axis, [(i, (i + step) % size) for i in range(size)])  21.9 us
    all_to_all x1, blocking collectives, body(): grams = lax.all_to_all(grams, 'span', 0, 0, tiled=True)  17.5 us
    all_to_all x1, blocking collectives, body(): grams = lax.all_to_all(grams, ('stream', 'depth'), 0, 0, tiled=True)  13.3 us
    ppermute x6, waiting for transfers between devices, move(): lax.ppermute(value, axis, [(i, (i + step) % size) for i in range(size)])  3.55 us
    pallas_call x1, Pallas kernels, body(): pl.pallas_call(compute_kernel, in_specs=[VMEM] * 8, out_specs=[VMEM] * 3,...  2.85 us
    pallas_call x1, Pallas kernels, body(): pl.pallas_call(functools.partial(basis_kernel, cells * span * others), in...  2.69 us
  transfers between devices with their start and end apart: 6, of which 1 were waited for; matrix products, arithmetic and copies ran while one was open for 0% of the time, Pallas kernels for 0%

profile of v6, /device:TPU:1, one launch (start us, length us, event | category | flops | bytes accessed | tf_op | source)
XLA Modules:
  0.0 63.4 jit_solution(7997584301279501309)
XLA Ops:
  0.0 1.3 %shard_map.37 = (f32[6,8,16,128]{3,2,1,0:T(8,128)S(1)}, f32[32,81]{1,0:T(8,128)S(1)}, f32[6,2,16,128]{3,2,1,0:T(8,128)S(1)}, f32[6,2,16,128]{3,2,1,0:T(8,128)S(1...) custom-call(f32[3,8,16,128]{3,2,1,0:T(8,128)} %f_hbm.1, ...), custom_call_target="tpu_custom_call" | custom-call | tf_op jit(solution)/shard_map/pallas_call | solution.py:236
  1.3 4.8 %collective-permute-start = (f32[6,2,16,128]{3,2,1,0:T(8,128)S(1)}, f32[6,2,16,128]{3,2,1,0:T(8,128)S(1)}, u32[]{:S(2)}, u32[]{:S(2)}) collective-permute-start(f32[6,2,16,128]{3,2,1,0:T(8,128)S(1)} %get-tuple-element.17), channel_id=1, source_target_pairs={{0,64},{64,128},{128,192},{192,256},{256,320},{320,384},{384,448},... | collective-permute-start | bytes 294920 | tf_op jit(solution)/shard_map/ppermute | solution.py:256
  6.1 8.6 %collective-permute-start.1 = (f32[6,2,16,128]{3,2,1,0:T(8,128)S(1)}, f32[6,2,16,128]{3,2,1,0:T(8,128)S(1)}, u32[]{:S(2)}, u32[]{:S(2)}) collective-permute-start(f32[6,2,16,128]{3,2,1,0:T(8,128)S(1)} %get-tuple-element.18), channel_id=1, source_target_pairs={{0,448},{64,0},{128,64},{192,128},{256,192},{320,256},{384,320},{4... | collective-permute-start | bytes 294920 | tf_op jit(solution)/shard_map/ppermute | solution.py:256
  14.7 2.1 %collective-permute-start.2 = (f32[6,8,2,128]{3,2,1,0:T(2,128)S(1)}, f32[6,8,2,128]{3,2,1,0:T(2,128)S(1)}, u32[]{:S(2)}, u32[]{:S(2)}) collective-permute-start(f32[6,8,2,128]{3,2,1,0:T(2,128)S(1)} %get-tuple-element.19), channel_id=1, source_target_pairs={{0,4},{4,8},{8,12},{12,16},{16,20},{20,24},{24,28},{28,32},{32,36}... | collective-permute-start | bytes 147464 | tf_op jit(solution)/shard_map/ppermute | solution.py:256
  16.8 0.0 collective-permute-start.3
  16.9 0.0 collective-permute-done.xb
  16.9 4.4 %collective-permute-start.5 = (f32[24,128]{1,0:T(8,128)S(1)}, f32[24,128]{1,0:T(8,128)S(1)}, u32[]{:S(2)}, u32[]{:S(2)}) collective-permute-start(f32[24,128]{1,0:T(8,128)S(1)} %get-tuple-element.22), channel_id=1, source_target_pairs={{0,3},{1,0},{2,1},{3,2},{4,7},{5,4},{6,5},{7,6},{8,11},{9,8},{10,9... | collective-permute-start | bytes 36872 | tf_op jit(solution)/shard_map/ppermute | solution.py:256
  21.2 1.9 %collective-permute-start.4 = (f32[24,128]{1,0:T(8,128)S(1)}, f32[24,128]{1,0:T(8,128)S(1)}, u32[]{:S(2)}, u32[]{:S(2)}) collective-permute-start(f32[24,128]{1,0:T(8,128)S(1)} %get-tuple-element.22), channel_id=1, source_target_pairs={{0,1},{1,2},{2,3},{3,0},{4,5},{5,6},{6,7},{7,4},{8,9},{9,10},{10,1... | collective-permute-start | bytes 36872 | tf_op jit(solution)/shard_map/ppermute | solution.py:256
  23.2 0.1 shard_map.38.wk_ref
  23.3 0.0 collective-permute-done.2.yb
  23.3 0.0 collective-permute-done.3.ya
  23.3 0.0 collective-permute-done.1.xa
  23.3 0.0 collective-permute-done.5.za
  23.3 3.5 %collective-permute-done.4.zb = f32[24,128]{1,0:T(8,128)S(1)} collective-permute-done((f32[24,128]{1,0:T(8,128)S(1)}, f32[24,128]{1,0:T(8,128)S(1)}, u32[]{:S(2)}, u32[]{:S(2)}) %collective-permute-start.4) | collective-permute-done | bytes 12320 | tf_op jit(solution)/shard_map/ppermute | solution.py:256
  26.9 2.8 %shard_map.39 = (bf16[32,16384]{1,0:T(8,128)(2,1)S(1)}, bf16[32,16384]{1,0:T(8,128)(2,1)S(1)}, f32[16,1,640]{2,1,0:T(1,128)S(1)}) custom-call(f32[6,8,16,128]{3,2,1,0:T(8,128)S(1)} %get-tuple-element.16.fields, f32[6,2,16,128]{3,2,1,0:T(8,128)S(1)} %collective-permute-done.xb, f32[6,2,16,128]{3,2,1,0:T(8,128)S(1)} %collective-permute-done.1.xa, ...), custom_call_target="tpu_custom_call" | custom-call | tf_op jit(solution)/shard_map/pallas_call | solution.py:274
  29.7 17.5 %all_to_all.10 = f32[16,1,640]{2,1,0:T(1,128)S(1)} all-to-all(f32[16,1,640]{2,1,0:T(1,128)S(1)} %get-tuple-element.24), channel_id=1, replica_groups=mesh['stream'=8,'span'=16,'depth'=4] {'span'}, dimensions={0} | all-to-all | bytes 81920 | tf_op jit(solution)/shard_map/all_to_all | solution.py:291
  47.4 13.3 %all_to_all.11.r_ref = f32[32,1,640]{2,1,0:T(1,128)S(1)} all-to-all(f32[32,1,640]{2,1,0:T(1,128)S(1)} %broadcast_in_dim.2), channel_id=1, replica_groups=mesh['stream'=8,'span'=16,'depth'=4] {'stream','depth'}, dimensions={0} | all-to-all | bytes 163840 | tf_op jit(solution)/shard_map/all_to_all | solution.py:293
  60.7 2.7 %shard_map.40 = f32[32,8,16,128]{3,2,1,0:T(8,128)} custom-call(f32[32,1,640]{2,1,0:T(1,128)S(1)} %all_to_all.11.r_ref, bf16[32,16384]{1,0:T(8,128)(2,1)S(1)} %get-tuple-element.25.sh_ref, bf16[32,16384]{1,0:T(8,128)(2,1)S(1)} %get-tuple-element.26.sl_ref), custom_call_target="tpu_custom_call" | custom-call | tf_op jit(solution)/shard_map/pallas_call | solution.py:295
  (2 shorter events, 0.1 us)
Async XLA Ops:
  1.3 15.6 %collective-permute-start = (f32[6,2,16,128]{3,2,1,0:T(8,128)S(1)}, f32[6,2,16,128]{3,2,1,0:T(8,128)S(1)}, u32[]{:S(2)}, u32[]{:S(2)}) collective-permute-start(f32[6,2,16,128]{3,2,1,0:T(8,128)S(1)} %get-tuple-element.17), channel_id=1, source_target_pairs={{0,64},{64,128},{128,192},{192,256},{256,320},{320,384},{384,448},... | collective-permute-start | bytes 294920 | tf_op jit(solution)/shard_map/ppermute | solution.py:256
  6.1 17.2 %collective-permute-start.1 = (f32[6,2,16,128]{3,2,1,0:T(8,128)S(1)}, f32[6,2,16,128]{3,2,1,0:T(8,128)S(1)}, u32[]{:S(2)}, u32[]{:S(2)}) collective-permute-start(f32[6,2,16,128]{3,2,1,0:T(8,128)S(1)} %get-tuple-element.18), channel_id=1, source_target_pairs={{0,448},{64,0},{128,64},{192,128},{256,192},{320,256},{384,320},{4... | collective-permute-start | bytes 294920 | tf_op jit(solution)/shard_map/ppermute | solution.py:256
  14.7 8.6 %collective-permute-start.2 = (f32[6,8,2,128]{3,2,1,0:T(2,128)S(1)}, f32[6,8,2,128]{3,2,1,0:T(2,128)S(1)}, u32[]{:S(2)}, u32[]{:S(2)}) collective-permute-start(f32[6,8,2,128]{3,2,1,0:T(2,128)S(1)} %get-tuple-element.19), channel_id=1, source_target_pairs={{0,4},{4,8},{8,12},{12,16},{16,20},{20,24},{24,28},{28,32},{32,36}... | collective-permute-start | bytes 147464 | tf_op jit(solution)/shard_map/ppermute | solution.py:256
  16.8 6.5 %collective-permute-start.3 = (f32[6,8,2,128]{3,2,1,0:T(2,128)S(1)}, f32[6,8,2,128]{3,2,1,0:T(2,128)S(1)}, u32[]{:S(2)}, u32[]{:S(2)}) collective-permute-start(f32[6,8,2,128]{3,2,1,0:T(2,128)S(1)} %get-tuple-element.20), channel_id=1, source_target_pairs={{0,60},{4,0},{8,4},{12,8},{16,12},{20,16},{24,20},{28,24},{32,28},... | collective-permute-start | bytes 147464 | tf_op jit(solution)/shard_map/ppermute | solution.py:256
  16.9 6.5 %collective-permute-start.5 = (f32[24,128]{1,0:T(8,128)S(1)}, f32[24,128]{1,0:T(8,128)S(1)}, u32[]{:S(2)}, u32[]{:S(2)}) collective-permute-start(f32[24,128]{1,0:T(8,128)S(1)} %get-tuple-element.22), channel_id=1, source_target_pairs={{0,3},{1,0},{2,1},{3,2},{4,7},{5,4},{6,5},{7,6},{8,11},{9,8},{10,9... | collective-permute-start | bytes 36872 | tf_op jit(solution)/shard_map/ppermute | solution.py:256
  21.2 5.7 %collective-permute-start.4 = (f32[24,128]{1,0:T(8,128)S(1)}, f32[24,128]{1,0:T(8,128)S(1)}, u32[]{:S(2)}, u32[]{:S(2)}) collective-permute-start(f32[24,128]{1,0:T(8,128)S(1)} %get-tuple-element.22), channel_id=1, source_target_pairs={{0,1},{1,2},{2,3},{3,0},{4,5},{5,6},{6,7},{7,4},{8,9},{9,10},{10,1... | collective-permute-start | bytes 36872 | tf_op jit(solution)/shard_map/ppermute | solution.py:256

commit v7 on v6

--- a/solution.py
+++ b/solution.py
@@ -204,15 +204,15 @@
     high = inverse.astype(BF16).astype(F32)
     low = inverse - high
     factor = high + pltpu.roll(high, snaps, 1)
-    factor = factor + pltpu.roll(low, 2 * snaps, 1) + pltpu.roll(low, 3 * snaps, 1)
-    factor = factor.astype(BF16)
+    factor = factor + pltpu.roll(low, 2 * snaps, 1)
+    factor = factor.astype(BF16)[:, 0 : 3 * snaps]
 
     flat = out_ref.reshape(planes * snaps * rows, cols)
     copies = []
     for plane in range(planes):
         part = slice(plane * rows * cols, (plane + 1) * rows * cols)
         both = jnp.concatenate([sh_ref[:, part], sl_ref[:, part]], 0)
-        out = dot(factor, jnp.concatenate([both, both], 0))
+        out = dot(factor, jnp.concatenate([both, sh_ref[:, part]], 0))
         for y in range(rows):
             flat[pl.ds(plane * snaps * rows + y, snaps, stride=rows), :] = out[:, cols * y : cols * y + cols]
         copy = pltpu.make_async_copy(out_ref.at[plane], o_hbm.at[:, plane], sems.at[plane])

time: 63.7 us -> 63.7 us (level)
  no operation moved by 1% of the time
where the time goes in v7:
time: 63.7 us; the launch traced here: 63.4 us
  blocking collectives  30.9 us (49%)
  starting transfers between devices  21.9 us (34%)
  Pallas kernels  6.94 us (11%)
  waiting for transfers between devices  3.55 us (6%)
    ppermute x6, starting transfers between devices, move(): lax.ppermute(value, axis, [(i, (i + step) % size) for i in range(size)])  21.9 us
    all_to_all x1, blocking collectives, body(): grams = lax.all_to_all(grams, 'span', 0, 0, tiled=True)  17.5 us
    all_to_all x1, blocking collectives, body(): grams = lax.all_to_all(grams, ('stream', 'depth'), 0, 0, tiled=True)  13.3 us
    ppermute x6, waiting for transfers between devices, move(): lax.ppermute(value, axis, [(i, (i + step) % size) for i in range(size)])  3.55 us
    pallas_call x1, Pallas kernels, body(): pl.pallas_call(compute_kernel, in_specs=[VMEM] * 8, out_specs=[VMEM] * 3,...  2.85 us
    pallas_call x1, Pallas kernels, body(): pl.pallas_call(functools.partial(basis_kernel, cells * span * others), in...  2.7 us
  transfers between devices with their start and end apart: 6, of which 1 were waited for; matrix products, arithmetic and copies ran while one was open for 0% of the time, Pallas kernels for 0%

profile of v7, /device:TPU:1, one launch (start us, length us, event | category | flops | bytes accessed | tf_op | source)
XLA Modules:
  0.0 63.4 jit_solution(2095456122513327388)
XLA Ops:
  0.0 1.3 %shard_map.37 = (f32[6,8,16,128]{3,2,1,0:T(8,128)S(1)}, f32[32,81]{1,0:T(8,128)S(1)}, f32[6,2,16,128]{3,2,1,0:T(8,128)S(1)}, f32[6,2,16,128]{3,2,1,0:T(8,128)S(1...) custom-call(f32[3,8,16,128]{3,2,1,0:T(8,128)} %f_hbm.1, ...), custom_call_target="tpu_custom_call" | custom-call | tf_op jit(solution)/shard_map/pallas_call | solution.py:236
  1.3 4.8 %collective-permute-start = (f32[6,2,16,128]{3,2,1,0:T(8,128)S(1)}, f32[6,2,16,128]{3,2,1,0:T(8,128)S(1)}, u32[]{:S(2)}, u32[]{:S(2)}) collective-permute-start(f32[6,2,16,128]{3,2,1,0:T(8,128)S(1)} %get-tuple-element.17), channel_id=1, source_target_pairs={{0,64},{64,128},{128,192},{192,256},{256,320},{320,384},{384,448},... | collective-permute-start | bytes 294920 | tf_op jit(solution)/shard_map/ppermute | solution.py:256
  6.1 8.6 %collective-permute-start.1 = (f32[6,2,16,128]{3,2,1,0:T(8,128)S(1)}, f32[6,2,16,128]{3,2,1,0:T(8,128)S(1)}, u32[]{:S(2)}, u32[]{:S(2)}) collective-permute-start(f32[6,2,16,128]{3,2,1,0:T(8,128)S(1)} %get-tuple-element.18), channel_id=1, source_target_pairs={{0,448},{64,0},{128,64},{192,128},{256,192},{320,256},{384,320},{4... | collective-permute-start | bytes 294920 | tf_op jit(solution)/shard_map/ppermute | solution.py:256
  14.7 2.1 %collective-permute-start.2 = (f32[6,8,2,128]{3,2,1,0:T(2,128)S(1)}, f32[6,8,2,128]{3,2,1,0:T(2,128)S(1)}, u32[]{:S(2)}, u32[]{:S(2)}) collective-permute-start(f32[6,8,2,128]{3,2,1,0:T(2,128)S(1)} %get-tuple-element.19), channel_id=1, source_target_pairs={{0,4},{4,8},{8,12},{12,16},{16,20},{20,24},{24,28},{28,32},{32,36}... | collective-permute-start | bytes 147464 | tf_op jit(solution)/shard_map/ppermute | solution.py:256
  16.8 0.0 collective-permute-start.3
  16.9 0.0 collective-permute-done.xb
  16.9 4.4 %collective-permute-start.5 = (f32[24,128]{1,0:T(8,128)S(1)}, f32[24,128]{1,0:T(8,128)S(1)}, u32[]{:S(2)}, u32[]{:S(2)}) collective-permute-start(f32[24,128]{1,0:T(8,128)S(1)} %get-tuple-element.22), channel_id=1, source_target_pairs={{0,3},{1,0},{2,1},{3,2},{4,7},{5,4},{6,5},{7,6},{8,11},{9,8},{10,9... | collective-permute-start | bytes 36872 | tf_op jit(solution)/shard_map/ppermute | solution.py:256
  21.2 1.9 %collective-permute-start.4 = (f32[24,128]{1,0:T(8,128)S(1)}, f32[24,128]{1,0:T(8,128)S(1)}, u32[]{:S(2)}, u32[]{:S(2)}) collective-permute-start(f32[24,128]{1,0:T(8,128)S(1)} %get-tuple-element.22), channel_id=1, source_target_pairs={{0,1},{1,2},{2,3},{3,0},{4,5},{5,6},{6,7},{7,4},{8,9},{9,10},{10,1... | collective-permute-start | bytes 36872 | tf_op jit(solution)/shard_map/ppermute | solution.py:256
  23.2 0.1 shard_map.38.wk_ref
  23.3 0.0 collective-permute-done.2.yb
  23.3 0.0 collective-permute-done.3.ya
  23.3 0.0 collective-permute-done.1.xa
  23.3 0.0 collective-permute-done.5.za
  23.3 3.5 %collective-permute-done.4.zb = f32[24,128]{1,0:T(8,128)S(1)} collective-permute-done((f32[24,128]{1,0:T(8,128)S(1)}, f32[24,128]{1,0:T(8,128)S(1)}, u32[]{:S(2)}, u32[]{:S(2)}) %collective-permute-start.4) | collective-permute-done | bytes 12320 | tf_op jit(solution)/shard_map/ppermute | solution.py:256
  26.9 2.8 %shard_map.39 = (bf16[32,16384]{1,0:T(8,128)(2,1)S(1)}, bf16[32,16384]{1,0:T(8,128)(2,1)S(1)}, f32[16,1,640]{2,1,0:T(1,128)S(1)}) custom-call(f32[6,8,16,128]{3,2,1,0:T(8,128)S(1)} %get-tuple-element.16.fields, f32[6,2,16,128]{3,2,1,0:T(8,128)S(1)} %collective-permute-done.xb, f32[6,2,16,128]{3,2,1,0:T(8,128)S(1)} %collective-permute-done.1.xa, ...), custom_call_target="tpu_custom_call" | custom-call | tf_op jit(solution)/shard_map/pallas_call | solution.py:274
  29.7 17.5 %all_to_all.10 = f32[16,1,640]{2,1,0:T(1,128)S(1)} all-to-all(f32[16,1,640]{2,1,0:T(1,128)S(1)} %get-tuple-element.24), channel_id=1, replica_groups=mesh['stream'=8,'span'=16,'depth'=4] {'span'}, dimensions={0} | all-to-all | bytes 81920 | tf_op jit(solution)/shard_map/all_to_all | solution.py:291
  47.4 13.3 %all_to_all.11.r_ref = f32[32,1,640]{2,1,0:T(1,128)S(1)} all-to-all(f32[32,1,640]{2,1,0:T(1,128)S(1)} %broadcast_in_dim.2), channel_id=1, replica_groups=mesh['stream'=8,'span'=16,'depth'=4] {'stream','depth'}, dimensions={0} | all-to-all | bytes 163840 | tf_op jit(solution)/shard_map/all_to_all | solution.py:293
  60.7 2.7 %shard_map.40 = f32[32,8,16,128]{3,2,1,0:T(8,128)} custom-call(f32[32,1,640]{2,1,0:T(1,128)S(1)} %all_to_all.11.r_ref, bf16[32,16384]{1,0:T(8,128)(2,1)S(1)} %get-tuple-element.25.sh_ref, bf16[32,16384]{1,0:T(8,128)(2,1)S(1)} %get-tuple-element.26.sl_ref), custom_call_target="tpu_custom_call" | custom-call | tf_op jit(solution)/shard_map/pallas_call | solution.py:295
  (2 shorter events, 0.1 us)
Async XLA Ops:
  1.3 15.6 %collective-permute-start = (f32[6,2,16,128]{3,2,1,0:T(8,128)S(1)}, f32[6,2,16,128]{3,2,1,0:T(8,128)S(1)}, u32[]{:S(2)}, u32[]{:S(2)}) collective-permute-start(f32[6,2,16,128]{3,2,1,0:T(8,128)S(1)} %get-tuple-element.17), channel_id=1, source_target_pairs={{0,64},{64,128},{128,192},{192,256},{256,320},{320,384},{384,448},... | collective-permute-start | bytes 294920 | tf_op jit(solution)/shard_map/ppermute | solution.py:256
  6.1 17.2 %collective-permute-start.1 = (f32[6,2,16,128]{3,2,1,0:T(8,128)S(1)}, f32[6,2,16,128]{3,2,1,0:T(8,128)S(1)}, u32[]{:S(2)}, u32[]{:S(2)}) collective-permute-start(f32[6,2,16,128]{3,2,1,0:T(8,128)S(1)} %get-tuple-element.18), channel_id=1, source_target_pairs={{0,448},{64,0},{128,64},{192,128},{256,192},{320,256},{384,320},{4... | collective-permute-start | bytes 294920 | tf_op jit(solution)/shard_map/ppermute | solution.py:256
  14.7 8.6 %collective-permute-start.2 = (f32[6,8,2,128]{3,2,1,0:T(2,128)S(1)}, f32[6,8,2,128]{3,2,1,0:T(2,128)S(1)}, u32[]{:S(2)}, u32[]{:S(2)}) collective-permute-start(f32[6,8,2,128]{3,2,1,0:T(2,128)S(1)} %get-tuple-element.19), channel_id=1, source_target_pairs={{0,4},{4,8},{8,12},{12,16},{16,20},{20,24},{24,28},{28,32},{32,36}... | collective-permute-start | bytes 147464 | tf_op jit(solution)/shard_map/ppermute | solution.py:256
  16.8 6.5 %collective-permute-start.3 = (f32[6,8,2,128]{3,2,1,0:T(2,128)S(1)}, f32[6,8,2,128]{3,2,1,0:T(2,128)S(1)}, u32[]{:S(2)}, u32[]{:S(2)}) collective-permute-start(f32[6,8,2,128]{3,2,1,0:T(2,128)S(1)} %get-tuple-element.20), channel_id=1, source_target_pairs={{0,60},{4,0},{8,4},{12,8},{16,12},{20,16},{24,20},{28,24},{32,28},... | collective-permute-start | bytes 147464 | tf_op jit(solution)/shard_map/ppermute | solution.py:256
  16.9 6.5 %collective-permute-start.5 = (f32[24,128]{1,0:T(8,128)S(1)}, f32[24,128]{1,0:T(8,128)S(1)}, u32[]{:S(2)}, u32[]{:S(2)}) collective-permute-start(f32[24,128]{1,0:T(8,128)S(1)} %get-tuple-element.22), channel_id=1, source_target_pairs={{0,3},{1,0},{2,1},{3,2},{4,7},{5,4},{6,5},{7,6},{8,11},{9,8},{10,9... | collective-permute-start | bytes 36872 | tf_op jit(solution)/shard_map/ppermute | solution.py:256
  21.2 5.7 %collective-permute-start.4 = (f32[24,128]{1,0:T(8,128)S(1)}, f32[24,128]{1,0:T(8,128)S(1)}, u32[]{:S(2)}, u32[]{:S(2)}) collective-permute-start(f32[24,128]{1,0:T(8,128)S(1)} %get-tuple-element.22), channel_id=1, source_target_pairs={{0,1},{1,2},{2,3},{3,0},{4,5},{5,6},{6,7},{7,4},{8,9},{9,10},{10,1... | collective-permute-start | bytes 36872 | tf_op jit(solution)/shard_map/ppermute | solution.py:256
